TPU v7x, 128 devices: a whole 4x4x4 slice. The times are simulated.
128 devices in a mesh: gx: 8 (over z, x_hi), gy: 4 (over y), gz: 4 (over x_lo, core).
Axes of the slice: x: 4 (x_hi: 2, x_lo: 2; x = x_hi * 2 + x_lo), y: 4, z: 4, core: 2. Of those that a mesh axis runs over, the one named last changes fastest.
Arguments:
- velocity: float32 [3, 128, 128, 512], P(None, 'gx', 'gy', 'gz'), may hold values from -5 to 5
- target_visc: bfloat16 [128, 128, 512], P('gx', 'gy', 'gz'), may hold values from 0.0099487305 to 0.29882812
- weight_in: bfloat16 [128, 10], replicated, may hold values from -2 to 2
- bias_in: float32 [128], replicated, may hold values from -3 to 3
- weight_mid: bfloat16 [128, 128], replicated, may hold values from -0.5 to 0.5
- bias_mid: float32 [128], replicated, may hold values from -3 to 3
- weight_out: bfloat16 [128], replicated, may hold values from -0.5 to 0.5
- patch_count: int32 [8, 4, 4], P('gx', 'gy', 'gz'), may hold values from 4 to 8, as said below
- patch_corner: int32 [8, 4, 4, 8, 3], P('gx', 'gy', 'gz'), may hold values from 0 to 112, as said below
- patch_dest: int32 [8, 4, 4, 8], P('gx', 'gy', 'gz'), may hold values from 0 to 3, as said below
Outputs:
- new_velocity: float32 [3, 128, 128, 512], P(None, 'gx', 'gy', 'gz')
- grad_weight_in: float32 [128, 10], replicated
- grad_bias_in: float32 [128], replicated
- grad_weight_mid: float32 [128, 128], replicated
- grad_bias_mid: float32 [128], replicated
- grad_weight_out: float32 [128], replicated
Inputs may be any that keep to these rules, and one draw needn't show every extreme that they name: `patch_count`: bricks at either wall have all 8 slots live; the others have at least half of them live. `patch_corner`: entries along the last dimension are the corner's offsets along the first, second and third grid dimension inside the brick, so that every patch of 16 cells a side lies inside its brick. `patch_dest`: each brick sends exactly 2 of its 8 slots to each trainer index k, live or not; trainer k of a gx index is the device with gy index k and gz index k.
All inputs are finite; a program needn't handle non-finite values.
Results may differ from a plain program's by a relative error of at most 0.0003.
Values may be sent and summed in bfloat16 or wider, within the bound.
No kernel may reach another device: no remote copies, remote signals or barrier semaphores. Data moves between devices by JAX's collectives and lax.ppermute only.
A program may use at most 64 MiB of HBM per device.

v0:
```python
import jax
import jax.numpy as jnp
from jax import lax
from jax.sharding import PartitionSpec as P

PATCH = 16
CAP = 2


time_step = 0.2
base_viscosity = 0.02
eddy_scale = 0.1
grad_gain = 20.0
norm_epsilon = 1e-06


def padded(cells, sides, width, closed):
    for axis, dim in sides:
        count = lax.axis_size(axis)
        ends = count if closed else count - 1
        head = lax.slice_in_dim(cells, 0, width, axis=dim)
        tail = lax.slice_in_dim(cells, cells.shape[dim] - width, cells.shape[dim], axis=dim)
        cells = jnp.concatenate(
            [
                lax.ppermute(tail, axis, [(i, (i + 1) % count) for i in range(ends)]),
                cells,
                lax.ppermute(head, axis, [((i + 1) % count, i) for i in range(ends)]),
            ],
            axis=dim,
        )
    return cells


def mlp_forward(features, weight_in, bias_in, weight_mid, bias_mid, weight_out):
    pre_one = jnp.dot(weight_in, features, preferred_element_type=jnp.float32) + bias_in[:, None]
    act_one = jnp.tanh(pre_one)
    hidden_one = act_one.astype(jnp.bfloat16)
    pre_two = (
        jnp.dot(weight_mid, hidden_one, preferred_element_type=jnp.float32) + bias_mid[:, None]
    )
    act_two = jnp.tanh(pre_two)
    hidden_two = act_two.astype(jnp.bfloat16)
    logit_out = jnp.dot(weight_out, hidden_two, preferred_element_type=jnp.float32)
    return (act_one, hidden_one, act_two, hidden_two, logit_out)


def eddy_field(flat_features, params, block_size):
    total_cells = flat_features.shape[1]

    def one_block(block_index):
        start = block_index * block_size
        piece = lax.dynamic_slice_in_dim(flat_features, start, block_size, 1)
        logit_out = mlp_forward(piece, *params)[4]
        return eddy_scale * jax.nn.softplus(logit_out)

    blocks = lax.map(one_block, jnp.arange(total_cells // block_size, dtype=jnp.int32))
    return blocks.reshape(total_cells)


def tendency(widened, params, wall_field, block_size):
    center = widened[:, 1:-1, 1:-1, 1:-1]
    diff_x = (widened[:, 2:, 1:-1, 1:-1] - widened[:, :-2, 1:-1, 1:-1]) * 0.5
    diff_y = (widened[:, 1:-1, 2:, 1:-1] - widened[:, 1:-1, :-2, 1:-1]) * 0.5
    diff_z = (widened[:, 1:-1, 1:-1, 2:] - widened[:, 1:-1, 1:-1, :-2]) * 0.5
    laplace = widened[:, 2:, 1:-1, 1:-1] + widened[:, :-2, 1:-1, 1:-1]
    laplace = laplace + widened[:, 1:-1, 2:, 1:-1] + widened[:, 1:-1, :-2, 1:-1]
    laplace = laplace + widened[:, 1:-1, 1:-1, 2:] + widened[:, 1:-1, 1:-1, :-2] - 6.0 * center
    features = jnp.concatenate([diff_x, diff_y, diff_z, wall_field], 0).astype(jnp.bfloat16)
    flat_features = features.reshape(features.shape[0], -1)
    eddy_visc = eddy_field(flat_features, params, block_size).reshape(center.shape[1:])
    advect = center[0][None] * diff_x + center[1][None] * diff_y + center[2][None] * diff_z
    section_rate = -advect + (base_viscosity + eddy_visc)[None] * laplace
    return (section_rate, features)


def mlp_grads(features, target, weight, params):
    weight_in, bias_in, weight_mid, bias_mid, weight_out = params
    act_one, hidden_one, act_two, hidden_two, logit_out = mlp_forward(features, *params)
    eddy_visc = eddy_scale * jax.nn.softplus(logit_out)
    delta_out = (
        weight * (eddy_visc - target.astype(jnp.float32)) * eddy_scale * jax.nn.sigmoid(logit_out)
    ).astype(jnp.bfloat16)
    grad_out = jnp.dot(hidden_two, delta_out, preferred_element_type=jnp.float32)
    delta_two = (
        weight_out.astype(jnp.float32)[:, None]
        * delta_out.astype(jnp.float32)[None, :]
        * (1.0 - act_two * act_two)
    ).astype(jnp.bfloat16)
    grad_mid = jnp.dot(delta_two, hidden_one.T, preferred_element_type=jnp.float32)
    bias_two = jnp.sum(delta_two.astype(jnp.float32), axis=1)
    back_one = jnp.dot(weight_mid.T, delta_two, preferred_element_type=jnp.float32)
    delta_one = (back_one * (1.0 - act_one * act_one)).astype(jnp.bfloat16)
    grad_in = jnp.dot(delta_one, features.T, preferred_element_type=jnp.float32)
    bias_one = jnp.sum(delta_one.astype(jnp.float32), axis=1)
    return (grad_in, bias_one, grad_mid, bias_two, grad_out)


def patch_grads(payload, live_flags, params):
    channels, patch_total, patch_cells = payload.shape
    feat_count = channels - 1

    def add_pair(block_index, running):
        start = (block_index * 2).astype(jnp.int32)
        pair_block = lax.dynamic_slice_in_dim(payload, start, 2, 1)
        alive_pair = lax.dynamic_slice_in_dim(live_flags, start, 2, 0)
        features = pair_block[:feat_count].reshape(feat_count, 2 * patch_cells)
        target = pair_block[feat_count].reshape(2 * patch_cells)
        weight = jnp.repeat(alive_pair, patch_cells)
        grad_terms = mlp_grads(features, target, weight, params)
        return tuple((earlier + addend for earlier, addend in zip(running, grad_terms)))

    initial = tuple((jnp.zeros(param.shape, jnp.float32) for param in params))
    return lax.fori_loop(0, patch_total // 2, add_pair, initial)


def slot_rank(targets):
    slot_order = jnp.arange(targets.shape[0], dtype=jnp.int32)
    same_target = (targets[:, None] == targets[None, :]) & (
        slot_order[None, :] < slot_order[:, None]
    )
    return jnp.sum(same_target.astype(jnp.int32), axis=1)


def sort_patches(local_patches, live_slots, position, row_count):
    picker = (jnp.arange(row_count, dtype=jnp.int32)[:, None] == position[None, :]).astype(
        jnp.bfloat16
    )
    ordered = jnp.einsum(
        "rs,csp->crp", picker, local_patches, preferred_element_type=jnp.float32
    ).astype(jnp.bfloat16)
    ordered_live = jnp.dot(picker.astype(jnp.float32), live_slots, precision=lax.Precision.HIGHEST)
    return (ordered, ordered_live)


def normalize(grads):
    square = jnp.float32(0.0)
    for running in grads:
        square = square + jnp.sum(running * running)
    factor_norm = grad_gain / jnp.sqrt(square + norm_epsilon)
    return tuple((running * factor_norm for running in grads))


def on_device(
    velocity,
    target_visc,
    weight_in,
    bias_in,
    weight_mid,
    bias_mid,
    weight_out,
    patch_count,
    patch_corner,
    patch_dest,
):
    params = (weight_in, bias_in, weight_mid, bias_mid, weight_out)
    components, size_x, size_y, size_z = velocity.shape
    cells_here = size_x * size_y * size_z
    block_size = min(8192, cells_here)
    rows_y = size_y * lax.axis_size("gy")
    y_global = (lax.axis_index("gy") * size_y + jnp.arange(size_y, dtype=jnp.int32)).astype(
        jnp.float32
    )
    wall_line = 1.0 - jnp.abs(2.0 * (y_global + 0.5) / rows_y - 1.0)
    wall_field = jnp.broadcast_to(wall_line[None, None, :, None], (1, size_x, size_y, size_z))

    def rates_of(field):
        widened = padded(field, (("gx", 1), ("gz", 3)), 1, True)
        widened = padded(widened, (("gy", 2),), 1, False)
        return tendency(widened, params, wall_field, block_size)

    rate_first, features = rates_of(velocity)
    first_section = velocity + time_step * rate_first
    rate_second, unused = rates_of(first_section)
    new_velocity = 0.5 * velocity + 0.5 * (first_section + time_step * rate_second)
    slot_total = patch_dest.shape[-1]
    live_total = patch_count.reshape(())
    corners = patch_corner.reshape(slot_total, 3)
    targets = patch_dest.reshape(slot_total)
    combined = jnp.concatenate([features, target_visc[None]], 0)
    channels = combined.shape[0]
    pieces = []
    for slot_index in range(slot_total):
        cube = lax.dynamic_slice(
            combined,
            (0, corners[slot_index, 0], corners[slot_index, 1], corners[slot_index, 2]),
            (channels, PATCH, PATCH, PATCH),
        )
        pieces.append(cube.reshape(channels, PATCH**3))
    local_patches = jnp.stack(pieces, 1)
    live_slots = (jnp.arange(slot_total, dtype=jnp.int32) < live_total).astype(jnp.float32)
    rank = slot_rank(targets)
    position = targets * CAP + rank
    outgoing, outgoing_live = sort_patches(local_patches, live_slots, position, slot_total)
    live_wire = outgoing_live.astype(jnp.bfloat16).reshape(1, slot_total, 1)
    spanned, spanned_live = (
        lax.all_to_all(outgoing, "gz", split_axis=1, concat_axis=1, tiled=True),
        lax.all_to_all(live_wire, "gz", split_axis=1, concat_axis=1, tiled=True),
    )
    received, received_live = (
        lax.all_gather(spanned, "gy", axis=1, tiled=True),
        lax.all_gather(spanned_live, "gy", axis=1, tiled=True),
    )
    live_flags = received_live.reshape(received_live.shape[1]).astype(jnp.float32)
    grads = patch_grads(received, live_flags, params)
    totals = lax.psum(normalize(grads), ("gx", "gz"))
    return (new_velocity, totals[0], totals[1], totals[2], totals[3], totals[4])


def solution(mesh):
    in_specs = (
        P(None, "gx", "gy", "gz"),
        P("gx", "gy", "gz"),
        P(),
        P(),
        P(),
        P(),
        P(),
        P("gx", "gy", "gz"),
        P("gx", "gy", "gz", None, None),
        P("gx", "gy", "gz", None),
    )
    out_specs = (P(None, "gx", "gy", "gz"), P(), P(), P(), P(), P())
    return jax.shard_map(
        on_device, mesh=mesh, in_specs=in_specs, out_specs=out_specs, check_vma=False
    )
```

profile of v0, /device:TPU:1, one launch (start us, length us, event | category | flops | bytes accessed | tf_op | source)
XLA Modules:
  0.0 608.1 jit_solution(6613204658472307933)
XLA Ops:
  10.9 4.6 all-to-all-start
  16.3 2.9 collective-permute-start.1
  19.2 3.6 collective-permute-start
  62.5 8.9 %all-reduce = bf16[32]{0:T(256)(128)(2,1)S(1)} all-reduce(bf16[32]{0:T(256)(128)(2,1)S(1)} %dynamic-update-slice), channel_id=1, replica_groups=mesh['gx'=8,'gy'=4,'gz'=4] {'gy'}, use_global_device_ids=true, to_apply=%add | all-reduce | flops 32 | bytes 128
  80.9 5.1 collective-permute-start.5
  100.5 60.9 %while.42 = (s32[]{:T(128)}, f32[8,8192]{1,0:T(8,128)S(1)}, s32[8]{0:T(128)S(1)}, bf16[10,65536]{1,0:T(8,128)(2,1)}, bf16[128,10]{0,1:T(8,128)(2,1)S(1)}, /*inde...) while((s32[]{:T(128)}, f32[8,8192]{1,0:T(8,128)S(1)}, ...), condition=%wide.region_1.2_spmd, body=%wide.region_0.1_spmd.sunk | while | flops 295755776 | bytes 4657095 | solution.py:56
  101.8 3.2 fusion.129
  105.0 2.9 fusion.130
  109.4 3.2 fusion.129
  112.6 2.9 fusion.130
  117.1 3.2 fusion.129
  120.2 2.9 fusion.130
  124.7 3.2 fusion.129
  127.9 2.9 fusion.130
  132.3 3.2 fusion.129
  135.5 2.9 fusion.130
  139.9 3.2 fusion.129
  143.1 2.9 fusion.130
  147.5 3.2 fusion.129
  150.7 2.9 fusion.130
  155.2 3.2 fusion.129
  158.3 2.9 fusion.130
  161.6 4.6 multiply_add_fusion
  167.7 3.8 collective-permute-start.6
  171.6 6.0 constant_dynamic-slice_fusion.1
  191.2 4.2 stack.3
  205.2 4.2 all-to-all-start.1
  235.5 73.2 %while.43 = (s32[]{:T(128)}, f32[8,8192]{1,0:T(8,128)}, s32[8]{0:T(128)S(1)}, bf16[10,65536]{1,0:T(8,128)(2,1)}, bf16[128,10]{0,1:T(8,128)(2,1)S(1)}, /*index=5*...) while((s32[]{:T(128)}, f32[8,8192]{1,0:T(8,128)}, ...), condition=%wide.region_3.4_spmd, body=%wide.region_2.3_spmd.sunk | while | flops 295755776 | bytes 4657095 | solution.py:56
  236.8 3.1 fusion.137
  239.9 3.0 fusion.138
  245.9 3.1 fusion.137
  249.1 3.0 fusion.138
  255.1 3.1 fusion.137
  258.2 3.0 fusion.138
  264.3 3.1 fusion.137
  267.4 3.0 fusion.138
  273.4 3.1 fusion.137
  276.6 2.9 fusion.138
  282.6 3.1 fusion.137
  285.7 2.9 fusion.138
  291.7 3.1 fusion.137
  294.8 2.9 fusion.138
  300.8 3.1 fusion.137
  304.0 2.9 fusion.138
  312.1 4.0 add_multiply_fusion
  316.1 181.6 %while.44 = (s32[]{:T(128)}, f32[128,10]{0,1:T(8,128)S(1)}, f32[128]{0:T(128)S(1)}, f32[128,128]{1,0:T(8,128)S(1)}, f32[128]{0:T(128)S(1)}, /*index=5*/f32[128]{...) while((s32[]{:T(128)}, f32[128,10]{0,1:T(8,128)S(1)}, ...), condition=%wide.region_8.9_spmd.clone, body=%wide.region_5.8_spmd.clone.sunk | while | flops 871541888 | bytes 46338336 | solution.py:113
  321.5 3.5 convert_reduce_fusion.5
  332.9 3.5 convert_reduce_fusion.5
  344.2 3.5 convert_reduce_fusion.5
  355.6 3.5 convert_reduce_fusion.5
  366.9 3.5 convert_reduce_fusion.5
  378.3 3.5 convert_reduce_fusion.5
  389.6 3.5 convert_reduce_fusion.5
  401.0 3.5 convert_reduce_fusion.5
  412.3 3.5 convert_reduce_fusion.5
  423.7 3.5 convert_reduce_fusion.5
  435.0 3.5 convert_reduce_fusion.5
  446.4 3.5 convert_reduce_fusion.5
  457.7 3.5 convert_reduce_fusion.5
  469.1 3.5 convert_reduce_fusion.5
  480.4 3.5 convert_reduce_fusion.5
  491.8 3.5 convert_reduce_fusion.5
  504.1 64.3 %all-reduce.1 = (f32[128,10]{0,1:T(8,128)}, f32[128]{0:T(128)}, f32[128]{0:T(128)}, f32[128]{0:T(128)}) all-reduce(f32[128,10]{0,1:T(8,128)S(1)} %broadcast_multiply_fusion.1, f32[128]{0:T(128)S(1)} %broadcast_multiply_fusion.4, f32[128]{0:T(128)S(1)} %broadcast_multiply_fusion.3, ...), channel_id=1, replica_groups=mesh['gx'=8,'gy'=4,'gz'=4] {'gx','gz'}, use_global_device_ids=true, to_apply=%region_14.15 | all-reduce | flops 1664 | bytes 13312 | tf_op jit(solution)/shard_map/psum | solution.py:205
  568.4 31.0 %all-reduce.4.cloned.1.call-done = f32[128,128]{1,0:T(8,128)} async-done(((f32[128,128]{1,0:T(8,128)}), f32[128,128]{1,0:T(8,128)}) %all-reduce.4.cloned.1.call-update) | async-done | bytes 65552 | tf_op jit(solution)/shard_map/psum | solution.py:205
  (563 shorter events, 245.6 us)
Async XLA Ops:
  7.2 19.0 %copy-start = (f32[3,16,32,128]{3,2,1,0:T(8,128)S(1)}, f32[3,16,32,128]{3,2,1,0:T(8,128)}, u32[]{:S(2)}) copy-start(f32[3,16,32,128]{3,2,1,0:T(8,128)} %param.16) | copy-start | bytes 2359300
  9.5 0.6 copy-start.40
  10.9 51.2 %all-to-all-start = ((bf16[1,8,1]{2,0,1:T(2,128)(2,1)}), bf16[1,8,1]{2,0,1:T(2,128)(2,1)S(1)}, u32[]{:S(2)}, u32[]{:S(2)}) async-start(bf16[1,8,1]{2,0,1:T(2,128)(2,1)} %copy.151), calls=%async_computation | async-start | bytes 8192 | tf_op jit(solution)/shard_map/all_to_all | solution.py:197
  16.3 9.9 %collective-permute-start.1 = (f32[3,1,32,128]{3,2,1,0:T(8,128)S(1)}, f32[3,1,32,128]{3,2,1,0:T(8,128)S(1)}, u32[]{:S(2)}, u32[]{:S(2)}) collective-permute-start(f32[3,1,32,128]{3,2,1,0:T(8,128)S(1)} %get-tuple-element.511), channel_id=1, source_target_pairs={{0,16},{16,32},{32,48},{48,64},{64,80},{80,96},{96,112},{112,0},{1... | collective-permute-start | bytes 147464 | tf_op jit(solution)/shard_map/ppermute | solution.py:25
  19.2 7.1 %collective-permute-start = (f32[3,1,32,128]{3,2,1,0:T(8,128)S(1)}, f32[3,1,32,128]{3,2,1,0:T(8,128)S(1)}, u32[]{:S(2)}, u32[]{:S(2)}) collective-permute-start(f32[3,1,32,128]{3,2,1,0:T(8,128)S(1)} %get-tuple-element.512), channel_id=1, source_target_pairs={{16,0},{32,16},{48,32},{64,48},{80,64},{96,80},{112,96},{0,112},{1... | collective-permute-start | bytes 147464 | tf_op jit(solution)/shard_map/ppermute | solution.py:27
  26.2 0.6 copy-start.18
  26.8 0.6 copy-start.20
  27.7 23.2 %copy-start.43 = (u32[128]{0:T(128)S(1)}, u32[128]{0:T(128)}, u32[]{:S(2)}) copy-start(u32[128]{0:T(128)} %constant.137) | copy-start | bytes 1540
  29.3 44.2 %collective-permute-start.3 = (f32[3,18,32,1]{2,1,3,0:T(8,128)S(1)}, f32[3,18,32,1]{2,1,3,0:T(8,128)S(1)}, u32[]{:S(2)}, u32[]{:S(2)}) collective-permute-start(f32[3,18,32,1]{2,1,3,0:T(8,128)S(1)} %copy.164), channel_id=1, source_target_pairs={{1,0},{2,1},{3,2},{0,3},{5,4},{6,5},{7,6},{4,7},{9,8},{10,9},{11,1... | collective-permute-start | bytes 20744 | tf_op jit(solution)/shard_map/ppermute | solution.py:27
  29.7 44.3 %collective-permute-start.2 = (f32[3,18,32,1]{2,1,3,0:T(8,128)}, f32[3,18,32,1]{2,1,3,0:T(8,128)S(1)}, u32[]{:S(2)}, u32[]{:S(2)}) collective-permute-start(f32[3,18,32,1]{2,1,3,0:T(8,128)} %copy.163), channel_id=1, source_target_pairs={{0,1},{1,2},{2,3},{3,0},{4,5},{5,6},{6,7},{7,4},{8,9},{9,10},{10,1... | collective-permute-start | bytes 20744 | tf_op jit(solution)/shard_map/ppermute | solution.py:25
  50.9 46.6 %copy-start.12 = (bf16[1,65536]{1,0:T(2,128)(2,1)}, bf16[1,65536]{1,0:T(2,128)(2,1)S(1)}, u32[]{:S(2)}) copy-start(bf16[1,65536]{1,0:T(2,128)(2,1)S(1)} %reshape.134) | copy-start | bytes 393220
  73.5 0.6 copy-start.26
  74.1 0.6 copy-start.28
  76.3 9.7 %copy-start.19 = (f32[3,1,32,128]{3,2,1,0:T(8,128)S(1)}, f32[3,1,32,128]{3,2,1,0:T(8,128)}, u32[]{:S(2)}) copy-start(f32[3,1,32,128]{3,2,1,0:T(8,128)} %copy-done.18) | copy-start | bytes 147460
  76.3 9.7 %copy-start.21 = (f32[3,1,32,128]{3,2,1,0:T(8,128)S(1)}, f32[3,1,32,128]{3,2,1,0:T(8,128)}, u32[]{:S(2)}) copy-start(f32[3,1,32,128]{3,2,1,0:T(8,128)} %copy-done.20) | copy-start | bytes 147460
  79.6 11.5 %collective-permute-start.4 = (f32[3,18,1,130]{3,1,2,0:T(8,128)}, f32[3,18,1,130]{3,1,2,0:T(8,128)}, u32[]{:S(2)}, u32[]{:S(2)}) collective-permute-start(f32[3,18,1,130]{3,1,2,0:T(8,128)} %get-tuple-element.487), channel_id=1, source_target_pairs={{4,0},{8,4},{12,8},{5,1},{9,5},{13,9},{6,2},{10,6},{14,10},{7,3},{... | collective-permute-start | bytes 84248 | tf_op jit(solution)/shard_map/ppermute | solution.py:27
  80.9 11.3 %collective-permute-start.5 = (f32[3,18,1,130]{3,1,2,0:T(8,128)}, f32[3,18,1,130]{3,1,2,0:T(8,128)}, u32[]{:S(2)}, u32[]{:S(2)}) collective-permute-start(f32[3,18,1,130]{3,1,2,0:T(8,128)} %get-tuple-element.488), channel_id=1, source_target_pairs={{0,4},{4,8},{8,12},{1,5},{5,9},{9,13},{2,6},{6,10},{10,14},{3,7},{... | collective-permute-start | bytes 84248 | tf_op jit(solution)/shard_map/ppermute | solution.py:25
  86.5 1.8 copy-start.29
  86.5 3.1 copy-start.27
  91.0 4.8 copy-start.6
  91.0 4.8 copy-start.7
  92.1 4.6 copy-start.14
  93.1 3.6 copy-start.15
  97.5 3.0 copy-start.8
  97.5 3.0 copy-start.31
  97.5 3.0 copy-start.32
  97.5 3.0 copy-start.35
  97.6 3.0 copy-start.38
  161.6 10.0 %copy-start.30 = (bf16[16,32,128]{2,1,0:T(8,128)(2,1)S(1)}, bf16[16,32,128]{2,1,0:T(8,128)(2,1)}, u32[]{:S(2)}) copy-start(bf16[16,32,128]{2,1,0:T(8,128)(2,1)} %param.17) | copy-start | bytes 393220
  166.2 30.3 %collective-permute-start.7 = (f32[3,1,32,128]{3,2,1,0:T(8,128)S(1)}, f32[3,1,32,128]{3,2,1,0:T(8,128)S(1)}, u32[]{:S(2)}, u32[]{:S(2)}) collective-permute-start(f32[3,1,32,128]{3,2,1,0:T(8,128)S(1)} %get-tuple-element.506), channel_id=1, source_target_pairs={{0,16},{16,32},{32,48},{48,64},{64,80},{80,96},{96,112},{112,0},{1... | collective-permute-start | bytes 147464 | tf_op jit(solution)/shard_map/ppermute | solution.py:25
  167.7 28.9 %collective-permute-start.6 = (f32[3,1,32,128]{3,2,1,0:T(8,128)S(1)}, f32[3,1,32,128]{3,2,1,0:T(8,128)S(1)}, u32[]{:S(2)}, u32[]{:S(2)}) collective-permute-start(f32[3,1,32,128]{3,2,1,0:T(8,128)S(1)} %get-tuple-element.507), channel_id=1, source_target_pairs={{16,0},{32,16},{48,32},{64,48},{80,64},{96,80},{112,96},{0,112},{1... | collective-permute-start | bytes 147464 | tf_op jit(solution)/shard_map/ppermute | solution.py:27
  177.5 11.5 %copy-start.11 = (bf16[11,16,16,16]{3,2,1,0:T(8,128)(2,1)S(1)}, bf16[11,16,16,16]{3,2,1,0:T(8,128)(2,1)}, u32[]{:S(2)}) copy-start(bf16[11,16,16,16]{3,2,1,0:T(8,128)(2,1)} %get-tuple-element.494) | copy-start | bytes 270340
  179.4 10.8 %copy-start.10 = (bf16[11,16,16,16]{3,2,1,0:T(8,128)(2,1)S(1)}, bf16[11,16,16,16]{3,2,1,0:T(8,128)(2,1)}, u32[]{:S(2)}) copy-start(bf16[11,16,16,16]{3,2,1,0:T(8,128)(2,1)} %get-tuple-element.495) | copy-start | bytes 270340
  190.2 5.2 copy-start.41
  196.6 0.6 copy-start.22
  197.2 0.6 copy-start.24
  199.3 4.6 copy-start.9
  199.8 11.6 %collective-permute-start.9 = (f32[3,18,32,1]{2,1,3,0:T(8,128)S(1)}, f32[3,18,32,1]{2,1,3,0:T(8,128)S(1)}, u32[]{:S(2)}, u32[]{:S(2)}) collective-permute-start(f32[3,18,32,1]{2,1,3,0:T(8,128)S(1)} %copy.166), channel_id=1, source_target_pairs={{1,0},{2,1},{3,2},{0,3},{5,4},{6,5},{7,6},{4,7},{9,8},{10,9},{11,1... | collective-permute-start | bytes 20744 | tf_op jit(solution)/shard_map/ppermute | solution.py:27
  202.2 9.7 %collective-permute-start.8 = (f32[3,18,32,1]{2,1,3,0:T(8,128)}, f32[3,18,32,1]{2,1,3,0:T(8,128)S(1)}, u32[]{:S(2)}, u32[]{:S(2)}) collective-permute-start(f32[3,18,32,1]{2,1,3,0:T(8,128)} %copy.165), channel_id=1, source_target_pairs={{0,1},{1,2},{2,3},{3,0},{4,5},{5,6},{6,7},{7,4},{8,9},{9,10},{10,1... | collective-permute-start | bytes 20744 | tf_op jit(solution)/shard_map/ppermute | solution.py:25
  205.2 26.7 %all-to-all-start.1 = ((bf16[11,8,4096]{2,0,1:T(8,128)(2,1)}), bf16[11,8,4096]{2,0,1:T(8,128)(2,1)}, u32[]{:S(2)}, u32[]{:S(2)}) async-start(bf16[11,8,4096]{2,0,1:T(8,128)(2,1)} %copy.160), calls=%async_computation.1 | async-start | bytes 2097152 | tf_op jit(solution)/shard_map/all_to_all | solution.py:196
  209.5 106.6 %all-gather.2.cloned.1.call-start = ((), (), s32[]{:S(2)}) async-start(), calls=%async_computation.2 | async-start | bytes 3604480 | tf_op jit(solution)/shard_map/all_gather | solution.py:200
  216.0 1.4 copy-start.2
  217.4 5.7 copy-start.23
  217.4 5.7 copy-start.25
  218.1 8.0 %collective-permute-start.11 = (f32[3,18,1,130]{3,1,2,0:T(8,128)}, f32[3,18,1,130]{3,1,2,0:T(8,128)}, u32[]{:S(2)}, u32[]{:S(2)}) collective-permute-start(f32[3,18,1,130]{3,1,2,0:T(8,128)} %get-tuple-element.485), channel_id=1, source_target_pairs={{0,4},{4,8},{8,12},{1,5},{5,9},{9,13},{2,6},{6,10},{10,14},{3,7},{... | collective-permute-start | bytes 84248 | tf_op jit(solution)/shard_map/ppermute | solution.py:25
  220.0 7.0 %collective-permute-start.10 = (f32[3,18,1,130]{3,1,2,0:T(8,128)}, f32[3,18,1,130]{3,1,2,0:T(8,128)}, u32[]{:S(2)}, u32[]{:S(2)}) collective-permute-start(f32[3,18,1,130]{3,1,2,0:T(8,128)} %get-tuple-element.486), channel_id=1, source_target_pairs={{4,0},{8,4},{12,8},{5,1},{9,5},{13,9},{6,2},{10,6},{14,10},{7,3},{... | collective-permute-start | bytes 84248 | tf_op jit(solution)/shard_map/ppermute | solution.py:27
  221.7 2.2 copy-start.4
  222.1 1.0 copy-start.5
  223.1 1.7 copy-start.3
  225.7 3.3 copy-start.13
  227.0 1.9 copy-start.16
  228.0 1.0 copy-start.17
  231.9 3.6 copy-start.36
  231.9 3.6 copy-start.39
  234.5 364.9 %all-reduce.4.cloned.1.call-start = ((), (), s32[]{:S(2)}) async-start(), calls=%async_computation.3 | async-start | bytes 131072 | tf_op jit(solution)/shard_map/psum | solution.py:205
  235.5 76.6 %copy-start.1 = (f32[3,16,32,128]{3,2,1,0:T(8,128)S(1)}, f32[3,16,32,128]{3,2,1,0:T(8,128)}, u32[]{:S(2)}) copy-start(f32[3,16,32,128]{3,2,1,0:T(8,128)} %param.16) | copy-start | bytes 2359300
  312.1 4.0 copy-start.33
  312.1 4.0 copy-start.34
  312.1 4.0 copy-start.37
  312.1 4.0 copy-start.42
Sparse Core Ops, SparseCore 0:
  234.6 35.1 all-gather.1
  504.2 95.1 all-reduce.3
where the time goes:
time: 617 us; the launch traced here: 608 us
  matrix products  179 us (29%)
  local copies, waits for them, and re-layouts  121 us (20%)
  other arithmetic  106 us (17%)
  blocking collectives  73.1 us (12%)
  between operations  49.4 us (8%)
  starting transfers between devices  35.7 us (6%)
  waiting for transfers between devices  31.1 us (5%)
  loops' own time  12.4 us (2%)
    psum x1, blocking collectives, on_device(): totals = lax.psum(normalize(grads), ('gx', 'gz'))  64.3 us
    dot_general x32, matrix products, mlp_forward(): jnp.dot(weight_in, features, preferred_element_type=jnp.float32)  64.1 us
    dot_general x32, matrix products, mlp_forward(): jnp.dot(weight_out, hidden_two, preferred_element_type=jnp.float32)  57.5 us
    reduce_sum x16, other arithmetic, mlp_grads(): bias_two = jnp.sum(delta_two.astype(jnp.float32), axis=1)  56 us
    psum x1, waiting for transfers between devices, on_device(): totals = lax.psum(normalize(grads), ('gx', 'gz'))  31 us
    slice x16, local copies, waits for them, and re-layouts, add_pair(): features = pair_block[:feat_count].reshape(feat_count, 2 * patch_cells)  20.4 us
    dot_general x16, matrix products, mlp_grads(): jnp.dot(weight_mid.T, delta_two, preferred_element_type=jnp.float32)  20 us
    another operation x9, local copies, waits for them, and re-layouts, on_device(): local_patches = jnp.stack(pieces, 1)  17.8 us
  transfers between devices with their start and end apart: 16, of which 1 were waited for; matrix products, arithmetic and copies ran while one was open for 22% of the time, Pallas kernels for 0%

commit v1 on v0

v1 whole, which is shorter than its diff:
```python
import jax
import jax.numpy as jnp
from jax import lax
from jax.experimental import pallas as pl
from jax.experimental.pallas import tpu as pltpu
from jax.sharding import PartitionSpec as P

SX, SY, SZ = 16, 32, 128
HID = 128
FEAT = 10
PATCH = 16
CAP = 2
TRAINERS = 4
SLOTS = CAP * TRAINERS
ROWS = 160
QROWS = ROWS // 4
WIDE = 2 * SZ

time_step = 0.2
base_viscosity = 0.02
eddy_scale = 0.1
grad_gain = 20.0
norm_epsilon = 1e-06

f32 = jnp.float32
bf16 = jnp.bfloat16


def lanes_of(shape):
    return lax.broadcasted_iota(jnp.int32, shape, len(shape) - 1)


def sublanes_of(shape):
    return lax.broadcasted_iota(jnp.int32, shape, len(shape) - 2)


def softplus(x):
    return jnp.maximum(x, 0.0) + jnp.log1p(jnp.exp(-jnp.abs(x)))


def sigmoid(x):
    e = jnp.exp(-jnp.abs(x))
    return jnp.where(x >= 0, 1.0, e) / (1.0 + e)


def dot(a, b):
    return lax.dot_general(a, b, (((1,), (0,)), ((), ())), preferred_element_type=f32)


def dot_nt(a, b):
    return lax.dot_general(a, b, (((1,), (1,)), ((), ())), preferred_element_type=f32)


def wall_plane(gy):
    rows = (gy * SY + sublanes_of((SY, SZ))).astype(f32)
    return 1.0 - jnp.abs(2.0 * (rows + 0.5) / (SY * 4) - 1.0)


def put_faces(x, planes, xlo, xhi, ylo, yhi, zlo, zhi):
    lane = lanes_of((SY, SZ))
    low, high = zlo[...], zhi[...]
    for c in range(3):
        plane = planes[c]
        ylo[c, pl.ds(x, 1), :] = plane[0:1]
        yhi[c, pl.ds(x, 1), :] = plane[SY - 1 : SY]
        here = lane == c * SX + x
        low = jnp.where(here, jnp.broadcast_to(plane[:, 0:1], (SY, SZ)), low)
        high = jnp.where(here, jnp.broadcast_to(plane[:, SZ - 1 : SZ], (SY, SZ)), high)
    zlo[...] = low
    zhi[...] = high


def faces_kernel(v, xlo, xhi, ylo, yhi, zlo, zhi):
    zlo[...] = jnp.zeros((SY, SZ), f32)
    zhi[...] = jnp.zeros((SY, SZ), f32)
    xlo[...] = v[:, 0]
    xhi[...] = v[:, SX - 1]

    def step(x, carry):
        put_faces(x, [v[c, x] for c in range(3)], xlo, xhi, ylo, yhi, zlo, zhi)
        return carry

    lax.fori_loop(0, SX, step, 0)


FACE_SHAPES = ((3, SY, SZ),) * 2 + ((3, SX, SZ),) * 2 + ((SY, SZ),) * 2


def face_structs():
    return [jax.ShapeDtypeStruct(s, f32) for s in FACE_SHAPES]


def whole(n):
    return [pl.BlockSpec(memory_space=pltpu.VMEM) for _ in range(n)]


def smem(n):
    return [pl.BlockSpec(memory_space=pltpu.SMEM) for _ in range(n)]


def pack_faces(v):
    return pl.pallas_call(
        faces_kernel, out_shape=face_structs(), in_specs=whole(1), out_specs=whole(6), name="faces"
    )(v)


def exchange(faces):
    xlo, xhi, ylo, yhi, zlo, zhi = faces

    def shift(low, high, axis, closed):
        count = lax.axis_size(axis)
        ends = count if closed else count - 1
        from_low = lax.ppermute(high, axis, [(i, (i + 1) % count) for i in range(ends)])
        from_high = lax.ppermute(low, axis, [((i + 1) % count, i) for i in range(ends)])
        return from_low, from_high

    return (
        shift(xlo, xhi, "gx", True) + shift(ylo, yhi, "gy", False) + shift(zlo, zhi, "gz", True)
    )


def fill_padded(v, halos, pad):
    hx0, hx1, hy0, hy1 = halos[:4]
    for c in range(3):
        pad[c, 0, 8 : 8 + SY] = hx0[c]
        pad[c, SX + 1, 8 : 8 + SY] = hx1[c]

    def step(x, carry):
        for c in range(3):
            pad[c, x + 1, 8 : 8 + SY] = v[c, x]
            pad[c, x + 1, 7:8] = hy0[c, pl.ds(x, 1), :]
            pad[c, x + 1, 8 + SY : 9 + SY] = hy1[c, pl.ds(x, 1), :]
        return carry

    lax.fori_loop(0, SX, step, 0)


def stencil(x, pad, hz0, hz1):
    lane = lanes_of((SY, SZ))
    low, high = hz0[...], hz1[...]
    centers, dxs, dys, dzs, laps = [], [], [], [], []
    for c in range(3):
        at = c * SX + x
        ctr = pad[c, x + 1, 8 : 8 + SY]
        xm, xp = pad[c, x, 8 : 8 + SY], pad[c, x + 2, 8 : 8 + SY]
        ym, yp = pad[c, x + 1, 7 : 7 + SY], pad[c, x + 1, 9 : 9 + SY]
        zm = jnp.where(lane == 0, pltpu.roll(low, (SZ - at) % SZ, 1), pltpu.roll(ctr, 1, 1))
        zp = jnp.where(
            lane == SZ - 1, pltpu.roll(high, SZ - 1 - at, 1), pltpu.roll(ctr, SZ - 1, 1)
        )
        centers.append(ctr)
        dxs.append((xp - xm) * 0.5)
        dys.append((yp - ym) * 0.5)
        dzs.append((zp - zm) * 0.5)
        laps.append(xp + xm + yp + ym + zp + zm - 6.0 * ctr)
    return centers, dxs, dys, dzs, laps


def columns(channels, group):
    parts = [ch[group * 8 : group * 8 + 8] for ch in channels]
    parts.append(jnp.ones((16, SZ), f32))
    return jnp.concatenate(parts, 0).astype(bf16)


def section_kernel(second, *refs):
    gy = refs[0]
    v, *halos = refs[1:8]
    at = 8
    if second:
        velocity = refs[at]
        at += 1
    first_w, mid_w, out_w = refs[at : at + 3]
    at += 3
    new = refs[at]
    at += 1
    if not second:
        faces = refs[at : at + 6]
        at += 6
    pad, h_one_s, h_two_s = refs[at : at + 3]
    fill_padded(v, halos, pad)
    wall = wall_plane(gy[0])
    h_one_s[HID : HID + 16] = jnp.ones((16, 16 * WIDE), bf16)
    if not second:
        faces[4][...] = jnp.zeros((SY, SZ), f32)
        faces[5][...] = jnp.zeros((SY, SZ), f32)

    def step(x, carry):
        centers, dxs, dys, dzs, laps = stencil(x, pad, halos[4], halos[5])
        diffs = dxs + dys + dzs
        for pair in range(2):
            operand = jnp.concatenate(
                [columns(diffs + [wall], 2 * pair), columns(diffs + [wall], 2 * pair + 1)], 1
            )
            for y in range(8):
                at = (pair * 8 + y) * WIDE
                pre = dot(first_w[y, 0:HID], operand)
                h_one_s[0:HID, at : at + WIDE] = jnp.tanh(pre.astype(bf16))
        for i in range(16):
            at = i * WIDE
            pre = dot(mid_w[...], h_one_s[:, at : at + WIDE])
            h_two_s[:, at : at + WIDE] = jnp.tanh(pre.astype(bf16))
        eddy = []
        for pair in range(2):
            logit = jnp.zeros((16, WIDE), f32)
            for y in range(8):
                at = (pair * 8 + y) * WIDE
                logit = logit + dot(out_w[y], h_two_s[:, at : at + WIDE])
            soft = eddy_scale * softplus(logit[:8])
            eddy += [soft[:, :SZ], soft[:, SZ:]]
        visc = base_viscosity + jnp.concatenate(eddy, 0)
        planes = []
        for c in range(3):
            advect = centers[0] * dxs[c] + centers[1] * dys[c] + centers[2] * dzs[c]
            moved = centers[c] + time_step * (visc * laps[c] - advect)
            if second:
                moved = 0.5 * velocity[c, x] + 0.5 * moved
            new[c, x] = moved
            planes.append(moved)
        if not second:
            put_faces(x, planes, *faces)
        return carry

    lax.fori_loop(0, SX, step, 0)
    if not second:
        faces[0][...] = new[:, 0]
        faces[1][...] = new[:, SX - 1]


def section(gy, v, halos, weights, velocity=None):
    second = velocity is not None
    outs = [jax.ShapeDtypeStruct((3, SX, SY, SZ), f32)]
    if not second:
        outs += face_structs()
    args = [gy, v, *halos] + ([velocity] if second else []) + list(weights)
    return pl.pallas_call(
        lambda *refs: section_kernel(second, *refs),
        out_shape=outs,
        in_specs=smem(1) + whole(len(args) - 1),
        out_specs=whole(len(outs)),
        scratch_shapes=[
            pltpu.VMEM((3, SX + 2, 48, SZ), f32),
            pltpu.VMEM((HID + 16, 16 * WIDE), bf16),
            pltpu.VMEM((HID, 16 * WIDE), bf16),
        ],
        name="section_two" if second else "section_one",
    )(*args)


def patch_kernel(
    gy, count, corner, dest, v, hx0, hx1, hy0, hy1, hz0, hz1, target,
    first_w, mid_w, out_w, mid_t, out_col, grads,
    tab, pad, feats, wall_s, tgt_s, h_one_s, h_two_s, d_one_s, d_two_s, f_s, d_s, row_s,
    acc_mid, acc_in, acc_out, stage,
):
    for t in range(TRAINERS):
        tab[3, t] = 0
    for s in range(SLOTS):
        d = dest[s]
        rank = tab[3, d]
        tab[3, d] = rank + 1
        spot = d * CAP + rank
        tab[0, spot] = corner[s, 1]
        tab[1, spot] = corner[s, 2]
        tab[2, spot] = jnp.where(s < count[0], 1, 0)
    wall_s[...] = wall_plane(gy[0])
    fill_padded(v, (hx0, hx1, hy0, hy1), pad)

    def plane(x, carry):
        _, dxs, dys, dzs, _ = stencil(x, pad, hz0, hz1)
        for i, diff in enumerate(dxs + dys + dzs):
            feats[i, x] = diff
        tgt_s[x] = target[x].astype(f32)
        return carry

    lax.fori_loop(0, SX, plane, 0)
    h_one_s[HID : HID + 16] = jnp.ones((16, 8 * WIDE), bf16)
    stage[...] = jnp.zeros((ROWS, SZ), f32)
    lane = lanes_of((PATCH, SZ))
    lane8 = lanes_of((8, WIDE))
    out_wide = out_col[...]

    def tile(i, carry):
        k = i // 4
        xo = i % 4

        @pl.when(xo == 0)
        def _():
            acc_mid[...] = jnp.zeros(acc_mid.shape, f32)
            acc_in[...] = jnp.zeros(acc_in.shape, f32)
            acc_out[...] = jnp.zeros(acc_out.shape, f32)

        chans = [jnp.zeros((PATCH, SZ), f32) for _ in range(11)]
        for q in range(8):
            xi, r = q // 2, q % 2
            spot = k * CAP + r
            cy, cz = tab[0, spot], tab[1, spot]
            x = xo * 4 + xi
            mine = lane // 16 == q
            turn = lax.rem(q * 16 - cz + SZ, SZ)
            for ch in range(11):
                if ch == 9:
                    piece = wall_s[pl.ds(cy, PATCH), :]
                elif ch == 10:
                    piece = tgt_s[x, pl.ds(cy, PATCH), :]
                else:
                    piece = feats[ch, x, pl.ds(cy, PATCH), :]
                if ch != 9:
                    piece = pltpu.roll(piece, turn, 1)
                chans[ch] = jnp.where(mine, piece, chans[ch])
        operand = jnp.concatenate([columns(chans[:10], 0), columns(chans[:10], 1)], 1)
        goal = jnp.concatenate([chans[10][:8], chans[10][8:]], 1)
        for y in range(8):
            at = y * WIDE
            pre = dot(first_w[y], operand)
            h_one_s[0:HID, at : at + WIDE] = jnp.tanh(pre[0:HID].astype(bf16))
            f_s[:, at : at + WIDE] = pre[HID : HID + 16].astype(bf16)
        for y in range(8):
            at = y * WIDE
            pre = dot(mid_w[...], h_one_s[:, at : at + WIDE])
            h_two_s[:, at : at + WIDE] = jnp.tanh(pre.astype(bf16))
        logit = jnp.zeros((16, WIDE), f32)
        for y in range(8):
            at = y * WIDE
            logit = logit + dot(out_w[y], h_two_s[:, at : at + WIDE])
        logit = logit[:8]
        live = jnp.where(
            (lane8 // 16) % 2 == 0, tab[2, k * CAP].astype(f32), tab[2, k * CAP + 1].astype(f32)
        )
        visc = eddy_scale * softplus(logit)
        delta = (live * (visc - goal) * eddy_scale * sigmoid(logit)).astype(bf16)
        row_s[...] = delta.astype(f32)
        for y in range(8):
            at = y * WIDE
            d_s[:, at : at + WIDE] = jnp.broadcast_to(row_s[y : y + 1], (16, WIDE)).astype(bf16)
            for half in range(2):
                to = at + half * SZ
                row = jnp.broadcast_to(row_s[y : y + 1, half * SZ : half * SZ + SZ], (HID, SZ))
                act = h_two_s[:, to : to + SZ].astype(f32)
                d_two_s[:, to : to + SZ] = (out_wide * row * (1.0 - act * act)).astype(bf16)
        acc_mid[...] += dot_nt(h_one_s[...], d_two_s[...])
        acc_out[...] += dot_nt(d_s[...], h_two_s[...])
        for y in range(8):
            at = y * WIDE
            back = dot(mid_t[...], d_two_s[:, at : at + WIDE])
            act = h_one_s[0:HID, at : at + WIDE].astype(f32)
            d_one_s[:, at : at + WIDE] = (back * (1.0 - act * act)).astype(bf16)
        acc_in[...] += dot_nt(f_s[...], d_one_s[...])

        @pl.when(xo == 3)
        def _():
            stage[0:HID] = acc_mid[0:HID]
            stage[HID : HID + 1] = acc_mid[HID : HID + 1]
            stage[HID + 1 : HID + 2] = acc_in[FEAT : FEAT + 1]
            stage[HID + 2 : HID + 3] = acc_out[0:1]
            stage[HID + 8 : HID + 8 + FEAT] = acc_in[0:FEAT]
            for q in range(4):
                grads[q, k] = stage[q * QROWS : (q + 1) * QROWS]

        return carry

    lax.fori_loop(0, 16, tile, 0)


def patch_grads(gy, count, corner, dest, v, halos, target, weights, mid_t, out_col):
    return pl.pallas_call(
        patch_kernel,
        out_shape=jax.ShapeDtypeStruct((4, TRAINERS, QROWS, SZ), f32),
        in_specs=smem(4) + whole(13),
        out_specs=pl.BlockSpec(memory_space=pltpu.VMEM),
        scratch_shapes=[
            pltpu.SMEM((4, 8), jnp.int32),
            pltpu.VMEM((3, SX + 2, 48, SZ), f32),
            pltpu.VMEM((9, SX, SY, SZ), f32),
            pltpu.VMEM((SY, SZ), f32),
            pltpu.VMEM((SX, SY, SZ), f32),
            pltpu.VMEM((HID + 16, 8 * WIDE), bf16),
            pltpu.VMEM((HID, 8 * WIDE), bf16),
            pltpu.VMEM((HID, 8 * WIDE), bf16),
            pltpu.VMEM((HID, 8 * WIDE), bf16),
            pltpu.VMEM((16, 8 * WIDE), bf16),
            pltpu.VMEM((16, 8 * WIDE), bf16),
            pltpu.VMEM((8, WIDE), f32),
            pltpu.VMEM((HID + 16, SZ), f32),
            pltpu.VMEM((16, SZ), f32),
            pltpu.VMEM((16, SZ), f32),
            pltpu.VMEM((ROWS, SZ), f32),
        ],
        name="patch_grads",
    )(gy, count, corner, dest, v, *halos, target, *weights, mid_t, out_col)


def gather_kernel(parts, out):
    total = parts[0]
    for i in range(1, 16):
        total = total + parts[i]
    square = jnp.sum(total * total)
    full = jnp.concatenate([total, jnp.zeros((SZ - QROWS, SZ), f32)], 0)
    out[...] = jnp.where(lanes_of((SZ, SZ)) == QROWS, square, full.T)


def scale_kernel(parts, out):
    x = parts[...].reshape(8, 2, 8, SZ)
    folded = x[:, 0] + x[:, 1]
    folded = folded.reshape(64, SZ)
    sub = sublanes_of((64, SZ))
    swapped = jnp.where(
        sub % 8 < 4, pltpu.roll(folded, 60, 0), pltpu.roll(folded, 4, 0)
    )
    norms = (folded + swapped)[:, QROWS : QROWS + 1]
    factor = jnp.broadcast_to(grad_gain / jnp.sqrt(norms + norm_epsilon), (64, SZ))
    scaled = x * factor.reshape(8, 1, 8, SZ)
    total = scaled[0]
    for i in range(1, 8):
        total = total + scaled[i]
    lane = lanes_of((1, SZ))
    quarters = []
    for q in range(4):
        rows = total[q // 2][(q % 2) * 4 : (q % 2) * 4 + 4]
        quarters.append(jnp.where(lane < QROWS, jnp.sum(rows, axis=0, keepdims=True), 0.0))
    left = quarters[0] + pltpu.roll(quarters[1], 40, 1) + pltpu.roll(quarters[2], 80, 1)
    tail = pltpu.roll(quarters[3], 120, 1)
    left = left + jnp.where(lane >= 120, tail, 0.0)
    right = jnp.where(lane < 32, tail, 0.0)
    out[...] = jnp.broadcast_to(jnp.concatenate([left, right], 1), (SZ, 2 * SZ))


def final_kernel(parts, mid, rest, rest_t):
    mid[...] = parts[:, 0:SZ]
    tail = parts[:, SZ : 2 * SZ]
    rest[...] = tail[:, 8 : 8 + FEAT]
    rest_t[...] = tail.T[0:8]


def call(kernel, outs, *args):
    return pl.pallas_call(
        kernel, out_shape=outs, in_specs=whole(len(args)),
        out_specs=jax.tree.map(lambda _: pl.BlockSpec(memory_space=pltpu.VMEM), outs),
        name=kernel.__name__,
    )(*args)


def struct(*shape):
    return jax.ShapeDtypeStruct(shape, f32)


def split_bias(bias):
    high = lax.reduce_precision(bias, 8, 7)
    middle = lax.reduce_precision(bias - high, 8, 7)
    low = bias - high - middle
    return jnp.stack([high, middle, low], 1).astype(bf16)


def prepare(weight_in, bias_in, weight_mid, bias_mid, weight_out):
    eye = jnp.eye(8, dtype=bf16)
    spread = (weight_in[None, :, :, None] * eye[:, None, None, :]).reshape(8, HID, FEAT * 8)
    bias = jnp.pad(split_bias(bias_in), ((0, 0), (0, 13)))
    first_w = jnp.concatenate([spread, jnp.broadcast_to(bias[None], (8, HID, 16))], 2)
    pick = jnp.eye(16, 11, dtype=bf16)[None, :, :, None] * jnp.concatenate(
        [jnp.broadcast_to(eye[:, None, None, :], (8, 1, FEAT, 8)),
         jnp.broadcast_to(eye[:1][:, None, None, :], (8, 1, 1, 8))], 2
    )
    pick = jnp.pad(pick.reshape(8, 16, 88), ((0, 0), (0, 0), (0, 8)))
    first_w = jnp.concatenate([first_w, pick], 1)
    mid_w = jnp.concatenate([weight_mid, jnp.pad(split_bias(bias_mid), ((0, 0), (0, 13)))], 1)
    out_w = jnp.pad(eye, ((0, 0), (0, 8)))[:, :, None] * weight_out[None, None, :]
    out_col = jnp.broadcast_to(weight_out.astype(f32)[:, None], (HID, SZ))
    return (first_w, mid_w, out_w), weight_mid.T, out_col


def on_device(
    velocity, target_visc, weight_in, bias_in, weight_mid, bias_mid, weight_out,
    patch_count, patch_corner, patch_dest,
):
    gy = lax.axis_index("gy").astype(jnp.int32).reshape(1)
    weights, mid_t, out_col = prepare(weight_in, bias_in, weight_mid, bias_mid, weight_out)
    halos = exchange(pack_faces(velocity))
    grads = patch_grads(
        gy, patch_count.reshape(1), patch_corner.reshape(SLOTS, 3), patch_dest.reshape(SLOTS),
        velocity, halos, target_visc, weights, mid_t, out_col,
    )
    every = ("gx", "gy", "gz")
    summed = lax.all_to_all(
        grads.reshape(16, QROWS, SZ), ("gy", "gz"), split_axis=0, concat_axis=0, tiled=True
    )
    velocity_late, grads = lax.optimization_barrier((velocity, grads))
    first, *faces = section(gy, velocity_late, halos, weights)
    summed, first = lax.optimization_barrier((summed, first))
    pieces = call(gather_kernel, struct(SZ, SZ), summed)
    pieces = lax.all_to_all(pieces, every, split_axis=0, concat_axis=0, tiled=True)
    halos = exchange(faces)
    pieces, halos = lax.optimization_barrier((pieces, halos))
    column = call(scale_kernel, struct(SZ, 2 * SZ), pieces)
    table = lax.all_to_all(column, every, split_axis=0, concat_axis=0, tiled=True)
    first, column = lax.optimization_barrier((first, column))
    (new_velocity,) = section(gy, first, halos, weights, velocity)
    table, new_velocity = lax.optimization_barrier((table, new_velocity))
    grad_mid, grad_in, rest = call(
        final_kernel, [struct(SZ, SZ), struct(SZ, FEAT), struct(8, SZ)], table
    )
    return (new_velocity, grad_in, rest[1], grad_mid, rest[0], rest[2])


def solution(mesh):
    in_specs = (
        P(None, "gx", "gy", "gz"),
        P("gx", "gy", "gz"),
        P(), P(), P(), P(), P(),
        P("gx", "gy", "gz"),
        P("gx", "gy", "gz", None, None),
        P("gx", "gy", "gz", None),
    )
    out_specs = (P(None, "gx", "gy", "gz"), P(), P(), P(), P(), P())
    return jax.shard_map(
        on_device, mesh=mesh, in_specs=in_specs, out_specs=out_specs, check_vma=False
    )
```

time: 617 us -> 148 us (0.24); the launches traced: 608 us -> 148 us
  matrix products: 179 us -> 0 us
  local copies, waits for them, and re-layouts: 121 us -> 11.3 us
  other arithmetic: 106 us -> 2.32 us
  Pallas kernels: 0 us -> 78.9 us
  blocking collectives: 73.1 us -> 0 us
  between operations: 49.4 us -> 1.66 us
  waiting for transfers between devices: 31.1 us -> 3.68 us
  starting transfers between devices: 35.7 us -> 49.8 us
  loops' own time: 12.4 us -> 0 us
    dot_general x146 -> x0, matrix products: 179 us -> none  [the longest x32 64.1 us: mlp_forward(): jnp.dot(weight_in, features, preferred_element_type=jnp.float32)]
    pallas_call x0 -> x7, Pallas kernels: none -> 78.9 us  [the longest x2 40.4 us: section(): pl.pallas_call(lambda *refs: section_kernel(second, *refs), out_shape=out...]
    psum x1 -> x0, blocking collectives: 64.3 us -> none  [on_device(): totals = lax.psum(normalize(grads), ('gx', 'gz'))]
    reduce_sum x21 -> x0, other arithmetic: 59.3 us -> none  [the longest x16 56 us: mlp_grads(): bias_two = jnp.sum(delta_two.astype(jnp.float32), axis=1)]
    psum x1 -> x0, waiting for transfers between devices: 31 us -> none  [on_device(): totals = lax.psum(normalize(grads), ('gx', 'gz'))]
    slice x23 -> x0, local copies, waits for them, and re-layouts: 23.9 us -> none  [the longest x16 20.4 us: add_pair(): features = pair_block[:feat_count].reshape(feat_count, 2 * patch_cells)]
    another operation x12 -> x1, local copies, waits for them, and re-layouts: 18.6 us -> 0.14 us  [split_bias(): return jnp.stack([high, middle, low], 1).astype(bf16)]
    dynamic_slice x33 -> x0, local copies, waits for them, and re-layouts: 17 us -> none  [the longest x16 9.75 us: eddy_field(): lax.map(one_block, jnp.arange(total_cells // block_size, dtype=jnp.int32))]
  transfers between devices with their start and end apart: 16 -> 15, of which waited for: 1 -> 2; matrix products, arithmetic and copies ran while one was open for 22% -> 3% of each run, Pallas kernels for 0% -> 27%
where the time goes in v1:
time: 148 us
  Pallas kernels  78.9 us (53%)
  starting transfers between devices  49.8 us (34%)
  local copies, waits for them, and re-layouts  11.3 us (8%)
  waiting for transfers between devices  3.68 us (2%)
  other arithmetic  2.32 us (2%)
  between operations  1.66 us (1%)
    pallas_call x2, Pallas kernels, section(): pl.pallas_call(lambda *refs: section_kernel(second, *refs), out_shape=out...  40.4 us
    pallas_call x1, Pallas kernels, patch_grads(): pl.pallas_call(patch_kernel, out_shape=jax.ShapeDtypeStruct((4, TRAINERS,...  30.1 us
    ppermute x6, starting transfers between devices, shift(): lax.ppermute(high, axis, [(i, (i + 1) % count) for i in range(ends)])  15.8 us
    all_to_all x1, starting transfers between devices, on_device(): lax.all_to_all(pieces, every, split_axis=0, concat_axis=0, tiled=True)  10.4 us
    ppermute x6, starting transfers between devices, shift(): lax.ppermute(low, axis, [((i + 1) % count, i) for i in range(ends)])  9.12 us
    all_to_all x1, starting transfers between devices, on_device(): lax.all_to_all(column, every, split_axis=0, concat_axis=0, tiled=True)  7.35 us
    all_to_all x1, starting transfers between devices, on_device(): lax.all_to_all(grads.reshape(16, QROWS, SZ), ('gy', 'gz'), split_axis=0,...  7.09 us
    unnamed x58, local copies, waits for them, and re-layouts  6.34 us
  transfers between devices with their start and end apart: 15, of which 2 were waited for; matrix products, arithmetic and copies ran while one was open for 3% of the time, Pallas kernels for 27%

profile of v1, /device:TPU:1, one launch (start us, length us, event | category | flops | bytes accessed | tf_op | source)
XLA Modules:
  0.0 147.6 jit_solution(124846259201558830)
XLA Ops:
  0.6 0.0 copy-start
  0.6 3.3 %faces.1 = (f32[3,32,128]{2,1,0:T(8,128)}, f32[3,32,128]{2,1,0:T(8,128)}, f32[3,16,128]{2,1,0:T(8,128)}, f32[3,16,128]{2,1,0:T(8,128)}, f32[32,128]{1,0:T(8,128)}, /*index=5*/f32[32,128]{1,0:T(8,128)}) custom-call(f32[3,16,32,128]{3,2,1,0:T(8,128)} %refs_8_.1), custom_call_target="tpu_custom_call" | custom-call | tf_op jit(solution)/shard_map/faces/pallas_call | solution.py:102
  4.0 2.6 %collective-permute-start.4 = (f32[32,128]{1,0:T(8,128)}, f32[32,128]{1,0:T(8,128)S(1)}, u32[]{:S(2)}, u32[]{:S(2)}) collective-permute-start(f32[32,128]{1,0:T(8,128)} %get-tuple-element.39), channel_id=1, source_target_pairs={{0,1},{1,2},{2,3},{3,0},{4,5},{5,6},{6,7},{7,4},{8,9},{9,10},{10,1... | collective-permute-start | bytes 49160 | tf_op jit(solution)/shard_map/ppermute | solution.py:113
  6.6 0.0 collective-permute-start.5
  6.6 3.2 %collective-permute-start.2 = (f32[3,16,128]{2,1,0:T(8,128)}, f32[3,16,128]{2,1,0:T(8,128)S(1)}, u32[]{:S(2)}, u32[]{:S(2)}) collective-permute-start(f32[3,16,128]{2,1,0:T(8,128)} %get-tuple-element.37), channel_id=1, source_target_pairs={{0,4},{4,8},{8,12},{1,5},{5,9},{9,13},{2,6},{6,10},{10,14},{3,7},{... | collective-permute-start | bytes 73736 | tf_op jit(solution)/shard_map/ppermute | solution.py:113
  9.8 1.3 collective-permute-start.3
  11.1 2.5 %collective-permute-start = (f32[3,32,128]{2,1,0:T(8,128)}, f32[3,32,128]{2,1,0:T(8,128)S(1)}, u32[]{:S(2)}, u32[]{:S(2)}) collective-permute-start(f32[3,32,128]{2,1,0:T(8,128)} %get-tuple-element.35), channel_id=1, source_target_pairs={{0,16},{16,32},{32,48},{48,64},{64,80},{80,96},{96,112},{112,0},{1... | collective-permute-start | bytes 147464 | tf_op jit(solution)/shard_map/ppermute | solution.py:113
  13.6 0.6 copy-done.18
  14.3 0.6 copy-done.19
  15.0 0.1 copy.35
  15.0 0.1 copy.33
  15.2 0.1 copy.44
  15.3 0.1 fusion.5
  15.5 0.1 mul.65
  15.6 0.1 mul.59
  15.7 0.6 copy-done.16
  16.2 0.7 broadcast_multiply_fusion.1.out_w.refs_10_.refs_11_
  17.0 0.0 copy-start.20
  17.0 0.8 fusion.1.first_w.refs_8_.refs_9_
  17.8 0.1 copy.36
  17.9 0.0 collective-permute-done.4.hz0.refs_6_
  17.9 3.6 %collective-permute-start.1 = (f32[3,32,128]{2,1,0:T(8,128)S(1)}, f32[3,32,128]{2,1,0:T(8,128)S(1)}, u32[]{:S(2)}, u32[]{:S(2)}) collective-permute-start(f32[3,32,128]{2,1,0:T(8,128)S(1)} %copy-done.20), channel_id=1, source_target_pairs={{16,0},{32,16},{48,32},{64,48},{80,64},{96,80},{112,96},{0,112},{1... | collective-permute-start | bytes 147464 | tf_op jit(solution)/shard_map/ppermute | solution.py:114
  21.5 0.6 fusion.6.mid_w.refs_9_.refs_10_
  22.2 0.0 copy-done.8
  22.2 0.7 copy.37
  23.5 0.0 copy-done.17
  23.6 0.7 copy.42
  24.2 0.0 collective-permute-done.5.hz1.refs_7_
  24.2 0.0 collective-permute-done.2.hy0.refs_4_
  24.3 0.0 collective-permute-done.3.hy1.refs_5_
  24.3 0.0 collective-permute-done.hx0.refs_2_
  24.3 0.0 collective-permute-done.1.hx1.refs_3_
  24.3 0.7 broadcast_in_dim.14.out_col
  25.1 30.1 %patch_grads.1 = f32[4,4,40,128]{3,2,1,0:T(8,128)} custom-call(s32[1]{0:T(128)} %bitcast.gy.refs_0_, s32[1]{0:T(128)} %bitcast.40.count, s32[8,3]{1,0:T(8,128)} %bitcast.47, s32[8]{0:T(128)} %bitcast.48, f32[3,16,32,128]{3,2,1,0:T(8,128)} %refs_8_.1, f32[3,32,128]{2,1,0:T(8,128)} %copy-done.3, f32[3,32,128]{2,1,0:T(8,128)} %copy-done.4, ...), custom_call_target="tpu_custom_call" | custom-call | tf_op jit(solution)/shard_map/patch_grads/pallas_call | solution.py:365
  55.2 7.1 %all-to-all-start = ((f32[16,40,128]{2,1,0:T(8,128)}), f32[16,40,128]{2,1,0:T(8,128)S(1)}, u32[]{:S(2)}, u32[]{:S(2)}) async-start(f32[16,40,128]{2,1,0:T(8,128)} %bitcast.41), calls=%async_computation | async-start | bytes 655360 | tf_op jit(solution)/shard_map/all_to_all | solution.py:482
  62.2 20.7 %section_one.1 = (f32[3,16,32,128]{3,2,1,0:T(8,128)}, f32[3,32,128]{2,1,0:T(8,128)}, f32[3,32,128]{2,1,0:T(8,128)}, f32[3,16,128]{2,1,0:T(8,128)}, f32[3,16,128]...) custom-call(s32[1]{0:T(128)} %bitcast.gy.refs_0_, f32[3,16,32,128]{3,2,1,0:T(8,128)} %refs_8_.1, ...), custom_call_target="tpu_custom_call" | custom-call | tf_op jit(solution)/shard_map/section_one/pallas_call | solution.py:235
  83.0 0.0 all-to-all-done.parts
  83.0 0.0 copy-start.1
  83.0 0.7 copy-done.1
  83.7 1.8 %gather_kernel.1 = f32[128,128]{1,0:T(8,128)} custom-call(f32[16,40,128]{2,1,0:T(8,128)} %copy-done.1), custom_call_target="tpu_custom_call" | custom-call | tf_op jit(solution)/shard_map/gather_kernel/pallas_call | solution.py:435
  85.5 10.4 %all-to-all-start.1 = ((f32[128,1,128]{2,1,0:T(1,128)}), f32[128,1,128]{2,1,0:T(1,128)S(1)}, u32[]{:S(2)}, u32[]{:S(2)}) async-start(f32[128,1,128]{2,1,0:T(1,128)} %bitcast.45), calls=%async_computation.1 | async-start | bytes 131072 | tf_op jit(solution)/shard_map/all_to_all | solution.py:489
  95.9 2.9 %collective-permute-start.6 = (f32[3,32,128]{2,1,0:T(8,128)S(1)}, f32[3,32,128]{2,1,0:T(8,128)S(1)}, u32[]{:S(2)}, u32[]{:S(2)}) collective-permute-start(f32[3,32,128]{2,1,0:T(8,128)S(1)} %copy-done.22), channel_id=1, source_target_pairs={{0,16},{16,32},{32,48},{48,64},{64,80},{80,96},{96,112},{112,0},{1... | collective-permute-start | bytes 147464 | tf_op jit(solution)/shard_map/ppermute | solution.py:113
  98.9 2.9 %collective-permute-start.7 = (f32[3,32,128]{2,1,0:T(8,128)S(1)}, f32[3,32,128]{2,1,0:T(8,128)S(1)}, u32[]{:S(2)}, u32[]{:S(2)}) collective-permute-start(f32[3,32,128]{2,1,0:T(8,128)S(1)} %copy-done.21), channel_id=1, source_target_pairs={{16,0},{32,16},{48,32},{64,48},{80,64},{96,80},{112,96},{0,112},{1... | collective-permute-start | bytes 147464 | tf_op jit(solution)/shard_map/ppermute | solution.py:114
  101.8 1.5 %collective-permute-start.10 = (f32[32,128]{1,0:T(8,128)S(1)}, f32[32,128]{1,0:T(8,128)S(1)}, u32[]{:S(2)}, u32[]{:S(2)}) collective-permute-start(f32[32,128]{1,0:T(8,128)S(1)} %copy-done.26), channel_id=1, source_target_pairs={{0,1},{1,2},{2,3},{3,0},{4,5},{5,6},{6,7},{7,4},{8,9},{9,10},{10,1... | collective-permute-start | bytes 49160 | tf_op jit(solution)/shard_map/ppermute | solution.py:113
  103.3 3.1 %collective-permute-start.8 = (f32[3,16,128]{2,1,0:T(8,128)S(1)}, f32[3,16,128]{2,1,0:T(8,128)S(1)}, u32[]{:S(2)}, u32[]{:S(2)}) collective-permute-start(f32[3,16,128]{2,1,0:T(8,128)S(1)} %copy-done.24), channel_id=1, source_target_pairs={{0,4},{4,8},{8,12},{1,5},{5,9},{9,13},{2,6},{6,10},{10,14},{3,7},{... | collective-permute-start | bytes 73736 | tf_op jit(solution)/shard_map/ppermute | solution.py:113
  106.4 1.3 collective-permute-start.9
  107.7 0.0 collective-permute-done.10.refs_6_
  107.7 0.1 collective-permute-start.11
  107.8 3.4 %collective-permute-done.11.refs_7_ = f32[32,128]{1,0:T(8,128)S(1)} collective-permute-done((f32[32,128]{1,0:T(8,128)S(1)}, f32[32,128]{1,0:T(8,128)S(1)}, u32[]{:S(2)}, u32[]{:S(2)}) %collective-permute-start.11) | collective-permute-done | bytes 16416 | tf_op jit(solution)/shard_map/ppermute | solution.py:114
  111.2 0.0 collective-permute-done.8.refs_4_
  111.2 0.2 collective-permute-done.9.refs_5_
  111.4 0.0 collective-permute-done.6.refs_2_
  111.4 0.0 collective-permute-done.7.refs_3_
  111.5 0.0 all-to-all-done.1
  111.5 0.6 copy-done.2
  112.1 1.7 %scale_kernel.1 = f32[128,256]{1,0:T(8,128)} custom-call(f32[128,128]{1,0:T(8,128)} %bitcast.44), custom_call_target="tpu_custom_call" | custom-call | tf_op jit(solution)/shard_map/scale_kernel/pallas_call | solution.py:435
  113.8 1.7 %copy.40 = f32[128,1,256]{2,1,0:T(1,128)} copy(f32[128,1,256]{2,0,1:T(8,128)} %bitcast.43) | data formatting | bytes 262144 | tf_op jit(solution)/shard_map/all_to_all | solution.py:493
  115.5 7.3 %all-to-all-start.2 = ((f32[128,1,256]{2,1,0:T(1,128)}), f32[128,1,256]{2,1,0:T(1,128)S(1)}, u32[]{:S(2)}, u32[]{:S(2)}) async-start(f32[128,1,256]{2,1,0:T(1,128)} %copy.40), calls=%async_computation.2 | async-start | bytes 262144 | tf_op jit(solution)/shard_map/all_to_all | solution.py:493
  122.9 19.6 %section_two.1 = f32[3,16,32,128]{3,2,1,0:T(8,128)} custom-call(s32[1]{0:T(128)} %bitcast.gy.refs_0_, f32[3,16,32,128]{3,2,1,0:T(8,128)} %get-tuple-element.52.refs_1_, f32[3,32,128]{2,1,0:T(8,128)} %copy-done.10, f32[3,32,128]{2,1,0:T(8,128)} %copy-done.11, f32[3,16,128]{2,1,0:T(8,128)} %copy-done.12, f32[3,16,128]{2,1,0:T(8,128)} %copy-done.13, ...), custom_call_target="tpu_custom_call" | custom-call | tf_op jit(solution)/shard_map/section_two/pallas_call | solution.py:235
  142.5 0.0 all-to-all-done.2
  142.5 0.7 copy.46
  143.2 1.6 %final_kernel.1 = (f32[128,128]{1,0:T(8,128)}, f32[128,10]{1,0:T(8,128)}, f32[8,128]{1,0:T(8,128)}) custom-call(f32[128,256]{1,0:T(8,128)} %bitcast.42), custom_call_target="tpu_custom_call" | custom-call | tf_op jit(solution)/shard_map/final_kernel/pallas_call | solution.py:435
  144.8 1.5 %copy.41 = f32[128,10]{0,1:T(8,128)} copy(f32[128,10]{1,0:T(8,128)} %get-tuple-element.77) | data formatting | bytes 10240
  146.3 1.3 slice_bitcast_fusion
  (60 shorter events, 0.2 us)
Async XLA Ops:
  0.6 14.4 %copy-start = (bf16[128,10]{0,1:T(8,128)(2,1)S(1)}, bf16[128,10]{0,1:T(8,128)(2,1)}, u32[]{:S(2)}) copy-start(bf16[128,10]{0,1:T(8,128)(2,1)} %param.12) | copy-start | bytes 7684
  4.0 13.9 %collective-permute-start.4 = (f32[32,128]{1,0:T(8,128)}, f32[32,128]{1,0:T(8,128)S(1)}, u32[]{:S(2)}, u32[]{:S(2)}) collective-permute-start(f32[32,128]{1,0:T(8,128)} %get-tuple-element.39), channel_id=1, source_target_pairs={{0,1},{1,2},{2,3},{3,0},{4,5},{5,6},{6,7},{7,4},{8,9},{9,10},{10,1... | collective-permute-start | bytes 49160 | tf_op jit(solution)/shard_map/ppermute | solution.py:113
  6.6 17.7 %collective-permute-start.5 = (f32[32,128]{1,0:T(8,128)}, f32[32,128]{1,0:T(8,128)S(1)}, u32[]{:S(2)}, u32[]{:S(2)}) collective-permute-start(f32[32,128]{1,0:T(8,128)} %get-tuple-element.40), channel_id=1, source_target_pairs={{1,0},{2,1},{3,2},{0,3},{5,4},{6,5},{7,6},{4,7},{9,8},{10,9},{11,1... | collective-permute-start | bytes 49160 | tf_op jit(solution)/shard_map/ppermute | solution.py:114
  6.6 17.7 %collective-permute-start.2 = (f32[3,16,128]{2,1,0:T(8,128)}, f32[3,16,128]{2,1,0:T(8,128)S(1)}, u32[]{:S(2)}, u32[]{:S(2)}) collective-permute-start(f32[3,16,128]{2,1,0:T(8,128)} %get-tuple-element.37), channel_id=1, source_target_pairs={{0,4},{4,8},{8,12},{1,5},{5,9},{9,13},{2,6},{6,10},{10,14},{3,7},{... | collective-permute-start | bytes 73736 | tf_op jit(solution)/shard_map/ppermute | solution.py:113
  9.8 14.5 %collective-permute-start.3 = (f32[3,16,128]{2,1,0:T(8,128)}, f32[3,16,128]{2,1,0:T(8,128)S(1)}, u32[]{:S(2)}, u32[]{:S(2)}) collective-permute-start(f32[3,16,128]{2,1,0:T(8,128)} %get-tuple-element.38), channel_id=1, source_target_pairs={{4,0},{8,4},{12,8},{5,1},{9,5},{13,9},{6,2},{10,6},{14,10},{7,3},{... | collective-permute-start | bytes 73736 | tf_op jit(solution)/shard_map/ppermute | solution.py:114
  11.1 13.2 %collective-permute-start = (f32[3,32,128]{2,1,0:T(8,128)}, f32[3,32,128]{2,1,0:T(8,128)S(1)}, u32[]{:S(2)}, u32[]{:S(2)}) collective-permute-start(f32[3,32,128]{2,1,0:T(8,128)} %get-tuple-element.35), channel_id=1, source_target_pairs={{0,16},{16,32},{32,48},{48,64},{64,80},{80,96},{96,112},{112,0},{1... | collective-permute-start | bytes 147464 | tf_op jit(solution)/shard_map/ppermute | solution.py:113
  13.6 0.7 copy-start.18
  14.3 0.7 copy-start.19
  15.6 0.7 copy-start.16
  17.0 1.0 copy-start.20
  17.8 3.7 %copy-start.5 = (bf16[128,128]{1,0:T(8,128)(2,1)S(1)}, bf16[128,128]{1,0:T(8,128)(2,1)}, u32[]{:S(2)}) copy-start(bf16[128,128]{1,0:T(8,128)(2,1)} %param.14) | copy-start | bytes 98308
  17.9 4.2 %copy-start.8 = (f32[32,128]{1,0:T(8,128)}, f32[32,128]{1,0:T(8,128)S(1)}, u32[]{:S(2)}) copy-start(f32[32,128]{1,0:T(8,128)S(1)} %collective-permute-done.4.hz0.refs_6_) | copy-start | bytes 49156
  17.9 6.4 %collective-permute-start.1 = (f32[3,32,128]{2,1,0:T(8,128)S(1)}, f32[3,32,128]{2,1,0:T(8,128)S(1)}, u32[]{:S(2)}, u32[]{:S(2)}) collective-permute-start(f32[3,32,128]{2,1,0:T(8,128)S(1)} %copy-done.20), channel_id=1, source_target_pairs={{16,0},{32,16},{48,32},{64,48},{80,64},{96,80},{112,96},{0,112},{1... | collective-permute-start | bytes 147464 | tf_op jit(solution)/shard_map/ppermute | solution.py:114
  22.9 0.7 copy-start.17
  24.2 0.8 copy-start.9
  24.2 0.8 copy-start.6
  24.3 0.8 copy-start.7
  24.3 0.8 copy-start.3
  24.3 0.7 copy-start.4
  55.2 27.8 %all-to-all-start = ((f32[16,40,128]{2,1,0:T(8,128)}), f32[16,40,128]{2,1,0:T(8,128)S(1)}, u32[]{:S(2)}, u32[]{:S(2)}) async-start(f32[16,40,128]{2,1,0:T(8,128)} %bitcast.41), calls=%async_computation | async-start | bytes 655360 | tf_op jit(solution)/shard_map/all_to_all | solution.py:482
  83.0 0.7 copy-start.1
  83.7 18.0 %copy-start.26 = (f32[32,128]{1,0:T(8,128)S(1)}, f32[32,128]{1,0:T(8,128)}, u32[]{:S(2)}) copy-start(f32[32,128]{1,0:T(8,128)} %get-tuple-element.48) | copy-start | bytes 49156
  83.7 19.6 %copy-start.24 = (f32[3,16,128]{2,1,0:T(8,128)S(1)}, f32[3,16,128]{2,1,0:T(8,128)}, u32[]{:S(2)}) copy-start(f32[3,16,128]{2,1,0:T(8,128)} %get-tuple-element.46) | copy-start | bytes 73732
  85.5 10.4 %copy-start.22 = (f32[3,32,128]{2,1,0:T(8,128)S(1)}, f32[3,32,128]{2,1,0:T(8,128)}, u32[]{:S(2)}) copy-start(f32[3,32,128]{2,1,0:T(8,128)} %get-tuple-element.44) | copy-start | bytes 147460
  85.5 13.4 %copy-start.21 = (f32[3,32,128]{2,1,0:T(8,128)S(1)}, f32[3,32,128]{2,1,0:T(8,128)}, u32[]{:S(2)}) copy-start(f32[3,32,128]{2,1,0:T(8,128)} %get-tuple-element.45) | copy-start | bytes 147460
  85.5 20.9 %copy-start.23 = (f32[3,16,128]{2,1,0:T(8,128)S(1)}, f32[3,16,128]{2,1,0:T(8,128)}, u32[]{:S(2)}) copy-start(f32[3,16,128]{2,1,0:T(8,128)} %get-tuple-element.47) | copy-start | bytes 73732
  85.5 22.2 %copy-start.25 = (f32[32,128]{1,0:T(8,128)S(1)}, f32[32,128]{1,0:T(8,128)}, u32[]{:S(2)}) copy-start(f32[32,128]{1,0:T(8,128)} %get-tuple-element.49) | copy-start | bytes 49156
  85.5 26.0 %all-to-all-start.1 = ((f32[128,1,128]{2,1,0:T(1,128)}), f32[128,1,128]{2,1,0:T(1,128)S(1)}, u32[]{:S(2)}, u32[]{:S(2)}) async-start(f32[128,1,128]{2,1,0:T(1,128)} %bitcast.45), calls=%async_computation.1 | async-start | bytes 131072 | tf_op jit(solution)/shard_map/all_to_all | solution.py:489
  95.9 15.5 %collective-permute-start.6 = (f32[3,32,128]{2,1,0:T(8,128)S(1)}, f32[3,32,128]{2,1,0:T(8,128)S(1)}, u32[]{:S(2)}, u32[]{:S(2)}) collective-permute-start(f32[3,32,128]{2,1,0:T(8,128)S(1)} %copy-done.22), channel_id=1, source_target_pairs={{0,16},{16,32},{32,48},{48,64},{64,80},{80,96},{96,112},{112,0},{1... | collective-permute-start | bytes 147464 | tf_op jit(solution)/shard_map/ppermute | solution.py:113
  98.9 12.6 %collective-permute-start.7 = (f32[3,32,128]{2,1,0:T(8,128)S(1)}, f32[3,32,128]{2,1,0:T(8,128)S(1)}, u32[]{:S(2)}, u32[]{:S(2)}) collective-permute-start(f32[3,32,128]{2,1,0:T(8,128)S(1)} %copy-done.21), channel_id=1, source_target_pairs={{16,0},{32,16},{48,32},{64,48},{80,64},{96,80},{112,96},{0,112},{1... | collective-permute-start | bytes 147464 | tf_op jit(solution)/shard_map/ppermute | solution.py:114
  101.8 5.9 %collective-permute-start.10 = (f32[32,128]{1,0:T(8,128)S(1)}, f32[32,128]{1,0:T(8,128)S(1)}, u32[]{:S(2)}, u32[]{:S(2)}) collective-permute-start(f32[32,128]{1,0:T(8,128)S(1)} %copy-done.26), channel_id=1, source_target_pairs={{0,1},{1,2},{2,3},{3,0},{4,5},{5,6},{6,7},{7,4},{8,9},{9,10},{10,1... | collective-permute-start | bytes 49160 | tf_op jit(solution)/shard_map/ppermute | solution.py:113
  103.3 8.0 %collective-permute-start.8 = (f32[3,16,128]{2,1,0:T(8,128)S(1)}, f32[3,16,128]{2,1,0:T(8,128)S(1)}, u32[]{:S(2)}, u32[]{:S(2)}) collective-permute-start(f32[3,16,128]{2,1,0:T(8,128)S(1)} %copy-done.24), channel_id=1, source_target_pairs={{0,4},{4,8},{8,12},{1,5},{5,9},{9,13},{2,6},{6,10},{10,14},{3,7},{... | collective-permute-start | bytes 73736 | tf_op jit(solution)/shard_map/ppermute | solution.py:113
  106.4 5.1 %collective-permute-start.9 = (f32[3,16,128]{2,1,0:T(8,128)S(1)}, f32[3,16,128]{2,1,0:T(8,128)S(1)}, u32[]{:S(2)}, u32[]{:S(2)}) collective-permute-start(f32[3,16,128]{2,1,0:T(8,128)S(1)} %copy-done.23), channel_id=1, source_target_pairs={{4,0},{8,4},{12,8},{5,1},{9,5},{13,9},{6,2},{10,6},{14,10},{7,3},{... | collective-permute-start | bytes 73736 | tf_op jit(solution)/shard_map/ppermute | solution.py:114
  107.7 6.1 %copy-start.14 = (f32[32,128]{1,0:T(8,128)}, f32[32,128]{1,0:T(8,128)S(1)}, u32[]{:S(2)}) copy-start(f32[32,128]{1,0:T(8,128)S(1)} %collective-permute-done.10.refs_6_) | copy-start | bytes 49156
  107.7 3.5 %collective-permute-start.11 = (f32[32,128]{1,0:T(8,128)S(1)}, f32[32,128]{1,0:T(8,128)S(1)}, u32[]{:S(2)}, u32[]{:S(2)}) collective-permute-start(f32[32,128]{1,0:T(8,128)S(1)} %copy-done.25), channel_id=1, source_target_pairs={{1,0},{2,1},{3,2},{0,3},{5,4},{6,5},{7,6},{4,7},{9,8},{10,9},{11,1... | collective-permute-start | bytes 49160 | tf_op jit(solution)/shard_map/ppermute | solution.py:114
  111.2 2.6 %copy-start.15 = (f32[32,128]{1,0:T(8,128)}, f32[32,128]{1,0:T(8,128)S(1)}, u32[]{:S(2)}) copy-start(f32[32,128]{1,0:T(8,128)S(1)} %collective-permute-done.11.refs_7_) | copy-start | bytes 49156
  111.2 2.6 %copy-start.12 = (f32[3,16,128]{2,1,0:T(8,128)}, f32[3,16,128]{2,1,0:T(8,128)S(1)}, u32[]{:S(2)}) copy-start(f32[3,16,128]{2,1,0:T(8,128)S(1)} %collective-permute-done.8.refs_4_) | copy-start | bytes 73732
  111.4 2.4 %copy-start.13 = (f32[3,16,128]{2,1,0:T(8,128)}, f32[3,16,128]{2,1,0:T(8,128)S(1)}, u32[]{:S(2)}) copy-start(f32[3,16,128]{2,1,0:T(8,128)S(1)} %collective-permute-done.9.refs_5_) | copy-start | bytes 73732
  111.4 4.1 %copy-start.10 = (f32[3,32,128]{2,1,0:T(8,128)}, f32[3,32,128]{2,1,0:T(8,128)S(1)}, u32[]{:S(2)}) copy-start(f32[3,32,128]{2,1,0:T(8,128)S(1)} %collective-permute-done.6.refs_2_) | copy-start | bytes 147460
  111.5 4.1 %copy-start.11 = (f32[3,32,128]{2,1,0:T(8,128)}, f32[3,32,128]{2,1,0:T(8,128)S(1)}, u32[]{:S(2)}) copy-start(f32[3,32,128]{2,1,0:T(8,128)S(1)} %collective-permute-done.7.refs_3_) | copy-start | bytes 147460
  111.5 0.7 copy-start.2
  115.5 27.0 %all-to-all-start.2 = ((f32[128,1,256]{2,1,0:T(1,128)}), f32[128,1,256]{2,1,0:T(1,128)S(1)}, u32[]{:S(2)}, u32[]{:S(2)}) async-start(f32[128,1,256]{2,1,0:T(1,128)} %copy.40), calls=%async_computation.2 | async-start | bytes 262144 | tf_op jit(solution)/shard_map/all_to_all | solution.py:493

commit v2 on v1

--- a/solution.py
+++ b/solution.py
@@ -15,6 +15,8 @@
 ROWS = 160
 QROWS = ROWS // 4
 WIDE = 2 * SZ
+GROUPS = 8
+STAGES = ("output", "middle", "input", "forward")
 
 time_step = 0.2
 base_viscosity = 0.02
@@ -169,14 +171,14 @@
     if second:
         velocity = refs[at]
         at += 1
-    first_w, mid_w, out_w = refs[at : at + 3]
+    first_w, mid_w, out_col = refs[at : at + 3]
     at += 3
     new = refs[at]
     at += 1
     if not second:
         faces = refs[at : at + 6]
         at += 6
-    pad, h_one_s, h_two_s = refs[at : at + 3]
+    pad, op_s, h_one_s, logit_s, adv_s, lap_s = refs[at : at + 6]
     fill_padded(v, halos, pad)
     wall = wall_plane(gy[0])
     h_one_s[HID : HID + 16] = jnp.ones((16, 16 * WIDE), bf16)
@@ -184,43 +186,57 @@
         faces[4][...] = jnp.zeros((SY, SZ), f32)
         faces[5][...] = jnp.zeros((SY, SZ), f32)
 
-    def step(x, carry):
+    def begin(x):
         centers, dxs, dys, dzs, laps = stencil(x, pad, halos[4], halos[5])
-        diffs = dxs + dys + dzs
-        for pair in range(2):
-            operand = jnp.concatenate(
-                [columns(diffs + [wall], 2 * pair), columns(diffs + [wall], 2 * pair + 1)], 1
-            )
-            for y in range(8):
-                at = (pair * 8 + y) * WIDE
-                pre = dot(first_w[y, 0:HID], operand)
-                h_one_s[0:HID, at : at + WIDE] = jnp.tanh(pre.astype(bf16))
-        for i in range(16):
-            at = i * WIDE
-            pre = dot(mid_w[...], h_one_s[:, at : at + WIDE])
-            h_two_s[:, at : at + WIDE] = jnp.tanh(pre.astype(bf16))
-        eddy = []
-        for pair in range(2):
-            logit = jnp.zeros((16, WIDE), f32)
-            for y in range(8):
-                at = (pair * 8 + y) * WIDE
-                logit = logit + dot(out_w[y], h_two_s[:, at : at + WIDE])
-            soft = eddy_scale * softplus(logit[:8])
-            eddy += [soft[:, :SZ], soft[:, SZ:]]
-        visc = base_viscosity + jnp.concatenate(eddy, 0)
+        chans = dxs + dys + dzs + [wall]
+        for group in range(4):
+            op_s[:, group * SZ : group * SZ + SZ] = columns(chans, group)
+        slot = x % 4
+        for c in range(3):
+            adv_s[slot, c] = centers[0] * dxs[c] + centers[1] * dys[c] + centers[2] * dzs[c]
+            lap_s[slot, c] = laps[c]
+
+    def finish(x, slot):
+        visc = base_viscosity + eddy_scale * softplus(logit_s[...])
         planes = []
         for c in range(3):
-            advect = centers[0] * dxs[c] + centers[1] * dys[c] + centers[2] * dzs[c]
-            moved = centers[c] + time_step * (visc * laps[c] - advect)
+            rate = visc * lap_s[slot, c] - adv_s[slot, c]
+            moved = pad[c, x + 1, 8 : 8 + SY] + time_step * rate
             if second:
                 moved = 0.5 * velocity[c, x] + 0.5 * moved
             new[c, x] = moved
             planes.append(moved)
         if not second:
             put_faces(x, planes, *faces)
+
+    def layer_one(i):
+        operand = op_s[:, i // 8 * WIDE : i // 8 * WIDE + WIDE]
+        pre = dot(first_w[i % 8, 0:HID], operand)
+        h_one_s[0:HID, i * WIDE : i * WIDE + WIDE] = jnp.tanh(pre.astype(bf16))
+
+    def layer_two(i):
+        pre = dot(mid_w[...], h_one_s[:, i * WIDE : i * WIDE + WIDE])
+        h_two = jnp.tanh(pre.astype(bf16)).astype(f32)
+        for half in range(2):
+            to = ((i // 8) * 2 + half) * 8 + i % 8
+            terms = h_two[:, half * SZ : half * SZ + SZ] * out_col[...]
+            logit_s[to : to + 1] = jnp.sum(terms, axis=0, keepdims=True)
+
+    begin(0)
+    for i in range(16):
+        layer_one(i)
+    begin(1)
+
+    def step(x, carry):
+        finish(jnp.maximum(x - 1, 0), (x + 3) % 4)
+        for i in range(16):
+            layer_two(i)
+            layer_one(i)
+        begin(jnp.minimum(x + 2, SX - 1))
         return carry
 
     lax.fori_loop(0, SX, step, 0)
+    finish(SX - 1, (SX - 1) % 4)
     if not second:
         faces[0][...] = new[:, 0]
         faces[1][...] = new[:, SX - 1]
@@ -239,8 +255,11 @@
         out_specs=whole(len(outs)),
         scratch_shapes=[
             pltpu.VMEM((3, SX + 2, 48, SZ), f32),
+            pltpu.VMEM((96, 4 * SZ), bf16),
             pltpu.VMEM((HID + 16, 16 * WIDE), bf16),
-            pltpu.VMEM((HID, 16 * WIDE), bf16),
+            pltpu.VMEM((SY, SZ), f32),
+            pltpu.VMEM((4, 3, SY, SZ), f32),
+            pltpu.VMEM((4, 3, SY, SZ), f32),
         ],
         name="section_two" if second else "section_one",
     )(*args)
@@ -249,7 +268,7 @@
 def patch_kernel(
     gy, count, corner, dest, v, hx0, hx1, hy0, hy1, hz0, hz1, target,
     first_w, mid_w, out_w, mid_t, out_col, grads,
-    tab, pad, feats, wall_s, tgt_s, h_one_s, h_two_s, d_one_s, d_two_s, f_s, d_s, row_s,
+    tab, pad, feats, wall_s, tgt_s, op_s, goal_s, h_one_s, h_two_s, d_one_s, d_two_s, f_s, d_s, row_s,
     acc_mid, acc_in, acc_out, stage,
 ):
     for t in range(TRAINERS):
@@ -279,16 +298,9 @@
     lane8 = lanes_of((8, WIDE))
     out_wide = out_col[...]
 
-    def tile(i, carry):
+    def assemble(i):
         k = i // 4
         xo = i % 4
-
-        @pl.when(xo == 0)
-        def _():
-            acc_mid[...] = jnp.zeros(acc_mid.shape, f32)
-            acc_in[...] = jnp.zeros(acc_in.shape, f32)
-            acc_out[...] = jnp.zeros(acc_out.shape, f32)
-
         chans = [jnp.zeros((PATCH, SZ), f32) for _ in range(11)]
         for q in range(8):
             xi, r = q // 2, q % 2
@@ -307,47 +319,99 @@
                 if ch != 9:
                     piece = pltpu.roll(piece, turn, 1)
                 chans[ch] = jnp.where(mine, piece, chans[ch])
-        operand = jnp.concatenate([columns(chans[:10], 0), columns(chans[:10], 1)], 1)
-        goal = jnp.concatenate([chans[10][:8], chans[10][8:]], 1)
-        for y in range(8):
-            at = y * WIDE
-            pre = dot(first_w[y], operand)
-            h_one_s[0:HID, at : at + WIDE] = jnp.tanh(pre[0:HID].astype(bf16))
-            f_s[:, at : at + WIDE] = pre[HID : HID + 16].astype(bf16)
-        for y in range(8):
-            at = y * WIDE
-            pre = dot(mid_w[...], h_one_s[:, at : at + WIDE])
-            h_two_s[:, at : at + WIDE] = jnp.tanh(pre.astype(bf16))
-        logit = jnp.zeros((16, WIDE), f32)
-        for y in range(8):
-            at = y * WIDE
-            logit = logit + dot(out_w[y], h_two_s[:, at : at + WIDE])
-        logit = logit[:8]
+        for half in range(2):
+            op_s[:, half * SZ : half * SZ + SZ] = columns(chans[:10], half)
+            goal_s[:, half * SZ : half * SZ + SZ] = chans[10][half * 8 : half * 8 + 8]
+
+    def layer_one(y):
+        at = y * WIDE
+        pre = dot(first_w[y], op_s[...])
+        h_one_s[0:HID, at : at + WIDE] = jnp.tanh(pre[0:HID].astype(bf16))
+        f_s[:, at : at + WIDE] = pre[HID : HID + 16].astype(bf16)
+
+    def layer_two(y):
+        at = y * WIDE
+        pre = dot(mid_w[...], h_one_s[:, at : at + WIDE])
+        h_two = jnp.tanh(pre.astype(bf16))
+        h_two_s[:, at : at + WIDE] = h_two
+        return dot(out_w[y], h_two)
+
+    def errors(k, logit):
         live = jnp.where(
             (lane8 // 16) % 2 == 0, tab[2, k * CAP].astype(f32), tab[2, k * CAP + 1].astype(f32)
         )
         visc = eddy_scale * softplus(logit)
-        delta = (live * (visc - goal) * eddy_scale * sigmoid(logit)).astype(bf16)
-        row_s[...] = delta.astype(f32)
-        for y in range(8):
-            at = y * WIDE
-            d_s[:, at : at + WIDE] = jnp.broadcast_to(row_s[y : y + 1], (16, WIDE)).astype(bf16)
-            for half in range(2):
-                to = at + half * SZ
-                row = jnp.broadcast_to(row_s[y : y + 1, half * SZ : half * SZ + SZ], (HID, SZ))
-                act = h_two_s[:, to : to + SZ].astype(f32)
-                d_two_s[:, to : to + SZ] = (out_wide * row * (1.0 - act * act)).astype(bf16)
-        acc_mid[...] += dot_nt(h_one_s[...], d_two_s[...])
-        acc_out[...] += dot_nt(d_s[...], h_two_s[...])
-        for y in range(8):
-            at = y * WIDE
-            back = dot(mid_t[...], d_two_s[:, at : at + WIDE])
-            act = h_one_s[0:HID, at : at + WIDE].astype(f32)
-            d_one_s[:, at : at + WIDE] = (back * (1.0 - act * act)).astype(bf16)
-        acc_in[...] += dot_nt(f_s[...], d_one_s[...])
-
-        @pl.when(xo == 3)
+        delta = live * (visc - goal_s[...]) * eddy_scale * sigmoid(logit)
+        row_s[...] = delta.astype(bf16).astype(f32)
+
+    def output_side(y):
+        at = y * WIDE
+        d_s[:, at : at + WIDE] = jnp.broadcast_to(row_s[y : y + 1], (16, WIDE)).astype(bf16)
+        for half in range(2):
+            to = at + half * SZ
+            row = jnp.broadcast_to(row_s[y : y + 1, half * SZ : half * SZ + SZ], (HID, SZ))
+            act = h_two_s[:, to : to + SZ].astype(f32)
+            d_two_s[:, to : to + SZ] = (out_wide * row * (1.0 - act * act)).astype(bf16)
+
+    def input_side(y):
+        at = y * WIDE
+        back = dot(mid_t[...], d_two_s[:, at : at + WIDE])
+        act = h_one_s[0:HID, at : at + WIDE].astype(f32)
+        d_one_s[:, at : at + WIDE] = (back * (1.0 - act * act)).astype(bf16)
+
+    def add_output(ys):
+        span = slice(ys[0] * WIDE, (ys[-1] + 1) * WIDE)
+        acc_mid[...] += dot_nt(h_one_s[:, span], d_two_s[:, span])
+        acc_out[...] += dot_nt(d_s[:, span], h_two_s[:, span])
+
+    def add_input(ys):
+        span = slice(ys[0] * WIDE, (ys[-1] + 1) * WIDE)
+        acc_in[...] += dot_nt(f_s[:, span], d_one_s[:, span])
+
+    assemble(0)
+    for y in range(8):
+        layer_one(y)
+    logit = jnp.zeros((16, WIDE), f32)
+    for y in range(8):
+        logit = logit + layer_two(y)
+    errors(0, logit[:8])
+    assemble(1)
+
+    def tile(i, carry):
+        @pl.when(i % 4 == 0)
         def _():
+            acc_mid[...] = jnp.zeros(acc_mid.shape, f32)
+            acc_in[...] = jnp.zeros(acc_in.shape, f32)
+            acc_out[...] = jnp.zeros(acc_out.shape, f32)
+
+        logit = jnp.zeros((16, WIDE), f32)
+        size = 8 // GROUPS
+        for step in range(GROUPS + 4):
+            for stage_at, work in enumerate(STAGES):
+                group = step - stage_at
+                if not 0 <= group < GROUPS:
+                    continue
+                ys = [group * size + j for j in range(size)]
+                if work == "output":
+                    for y in ys:
+                        output_side(y)
+                elif work == "middle":
+                    for y in ys:
+                        input_side(y)
+                    add_output(ys)
+                elif work == "input":
+                    add_input(ys)
+                    for y in ys:
+                        layer_one(y)
+                else:
+                    for y in ys:
+                        logit = logit + layer_two(y)
+        errors(jnp.minimum(i + 1, 15) // 4, logit[:8])
+        assemble(jnp.minimum(i + 2, 15))
+
+        @pl.when(i % 4 == 3)
+        def _():
+            k = i // 4
             stage[0:HID] = acc_mid[0:HID]
             stage[HID : HID + 1] = acc_mid[HID : HID + 1]
             stage[HID + 1 : HID + 2] = acc_in[FEAT : FEAT + 1]
@@ -373,6 +437,8 @@
             pltpu.VMEM((9, SX, SY, SZ), f32),
             pltpu.VMEM((SY, SZ), f32),
             pltpu.VMEM((SX, SY, SZ), f32),
+            pltpu.VMEM((96, WIDE), bf16),
+            pltpu.VMEM((8, WIDE), f32),
             pltpu.VMEM((HID + 16, 8 * WIDE), bf16),
             pltpu.VMEM((HID, 8 * WIDE), bf16),
             pltpu.VMEM((HID, 8 * WIDE), bf16),
@@ -421,14 +487,17 @@
     tail = pltpu.roll(quarters[3], 120, 1)
     left = left + jnp.where(lane >= 120, tail, 0.0)
     right = jnp.where(lane < 32, tail, 0.0)
-    out[...] = jnp.broadcast_to(jnp.concatenate([left, right], 1), (SZ, 2 * SZ))
-
-
-def final_kernel(parts, mid, rest, rest_t):
+    row = jnp.concatenate([left, right], 1)
+    out[...] = jnp.broadcast_to(row.reshape(1, 1, 2 * SZ), (SZ, 1, 2 * SZ))
+
+
+def final_kernel(parts, mid, rest_in, bias_in, bias_mid, rest_out):
     mid[...] = parts[:, 0:SZ]
-    tail = parts[:, SZ : 2 * SZ]
-    rest[...] = tail[:, 8 : 8 + FEAT]
-    rest_t[...] = tail.T[0:8]
+    tail = parts[:, SZ : 2 * SZ].T
+    bias_mid[...] = tail[0:1]
+    bias_in[...] = tail[1:2]
+    rest_out[...] = tail[2:3]
+    rest_in[...] = tail[8 : 8 + FEAT]
 
 
 def call(kernel, outs, *args):
@@ -443,28 +512,51 @@
     return jax.ShapeDtypeStruct(shape, f32)
 
 
-def split_bias(bias):
-    high = lax.reduce_precision(bias, 8, 7)
-    middle = lax.reduce_precision(bias - high, 8, 7)
+def bias_rows(bias):
+    high = bias.astype(bf16).astype(f32)
+    middle = (bias - high).astype(bf16).astype(f32)
     low = bias - high - middle
-    return jnp.stack([high, middle, low], 1).astype(bf16)
+    sub = sublanes_of((16, HID))
+    rows = jnp.where(sub == 0, high, jnp.where(sub == 1, middle, jnp.where(sub == 2, low, 0.0)))
+    return rows.astype(bf16)
+
+
+def one_hot(shape, test):
+    return jnp.where(test(sublanes_of(shape), lanes_of(shape)), 1.0, 0.0).astype(bf16)
+
+
+def prepare_kernel(w_in, b_in, w_mid, b_mid, w_out, first_w, mid_w, mid_t, out_w, out_col):
+    eye = one_hot((HID, HID), lambda i, j: i == j)
+    bias = dot_nt(eye, bias_rows(b_in[...])).astype(bf16)
+    bias_part = dot(bias, one_hot((16, 96), lambda i, j: j == 80 + i))
+    row = jnp.broadcast_to(w_out[...], (16, HID))
+    sub = sublanes_of((16, HID))
+    for y in range(8):
+        spread = one_hot((FEAT, 96), lambda i, j: j == i * 8 + y)
+        first_w[y, 0:HID] = (dot(w_in[...], spread) + bias_part).astype(bf16)
+        first_w[y, HID : HID + 16] = one_hot(
+            (16, 96),
+            lambda i, j: ((i < FEAT) & (j == i * 8 + y)) | ((i == FEAT) & (j == FEAT * 8)),
+        )
+        out_w[y] = jnp.where(sub == y, row.astype(f32), 0.0).astype(bf16)
+    mid_w[:, 0:HID] = w_mid[...]
+    mid_w[:, HID : HID + 16] = dot_nt(eye, bias_rows(b_mid[...])).astype(bf16)
+    mid_t[...] = dot_nt(eye, w_mid[...]).astype(bf16)
+    out_col[...] = dot_nt(eye, jnp.broadcast_to(w_out[...], (HID, HID)))
 
 
 def prepare(weight_in, bias_in, weight_mid, bias_mid, weight_out):
-    eye = jnp.eye(8, dtype=bf16)
-    spread = (weight_in[None, :, :, None] * eye[:, None, None, :]).reshape(8, HID, FEAT * 8)
-    bias = jnp.pad(split_bias(bias_in), ((0, 0), (0, 13)))
-    first_w = jnp.concatenate([spread, jnp.broadcast_to(bias[None], (8, HID, 16))], 2)
-    pick = jnp.eye(16, 11, dtype=bf16)[None, :, :, None] * jnp.concatenate(
-        [jnp.broadcast_to(eye[:, None, None, :], (8, 1, FEAT, 8)),
-         jnp.broadcast_to(eye[:1][:, None, None, :], (8, 1, 1, 8))], 2
-    )
-    pick = jnp.pad(pick.reshape(8, 16, 88), ((0, 0), (0, 0), (0, 8)))
-    first_w = jnp.concatenate([first_w, pick], 1)
-    mid_w = jnp.concatenate([weight_mid, jnp.pad(split_bias(bias_mid), ((0, 0), (0, 13)))], 1)
-    out_w = jnp.pad(eye, ((0, 0), (0, 8)))[:, :, None] * weight_out[None, None, :]
-    out_col = jnp.broadcast_to(weight_out.astype(f32)[:, None], (HID, SZ))
-    return (first_w, mid_w, out_w), weight_mid.T, out_col
+    outs = [
+        jax.ShapeDtypeStruct((8, HID + 16, 96), bf16),
+        jax.ShapeDtypeStruct((HID, HID + 16), bf16),
+        jax.ShapeDtypeStruct((HID, HID), bf16),
+        jax.ShapeDtypeStruct((8, 16, HID), bf16),
+        struct(HID, SZ),
+    ]
+    return call(
+        prepare_kernel, outs, weight_in, bias_in.reshape(1, HID), weight_mid,
+        bias_mid.reshape(1, HID), weight_out.reshape(1, HID),
+    )
 
 
 def on_device(
@@ -472,32 +564,40 @@
     patch_count, patch_corner, patch_dest,
 ):
     gy = lax.axis_index("gy").astype(jnp.int32).reshape(1)
-    weights, mid_t, out_col = prepare(weight_in, bias_in, weight_mid, bias_mid, weight_out)
+    first_w, mid_w, mid_t, out_w, out_col = prepare(
+        weight_in, bias_in, weight_mid, bias_mid, weight_out
+    )
+    net = (first_w, mid_w, out_col)
     halos = exchange(pack_faces(velocity))
     grads = patch_grads(
         gy, patch_count.reshape(1), patch_corner.reshape(SLOTS, 3), patch_dest.reshape(SLOTS),
-        velocity, halos, target_visc, weights, mid_t, out_col,
+        velocity, halos, target_visc, (first_w, mid_w, out_w), mid_t, out_col,
     )
     every = ("gx", "gy", "gz")
     summed = lax.all_to_all(
         grads.reshape(16, QROWS, SZ), ("gy", "gz"), split_axis=0, concat_axis=0, tiled=True
     )
     velocity_late, grads = lax.optimization_barrier((velocity, grads))
-    first, *faces = section(gy, velocity_late, halos, weights)
+    first, *faces = section(gy, velocity_late, halos, net)
     summed, first = lax.optimization_barrier((summed, first))
     pieces = call(gather_kernel, struct(SZ, SZ), summed)
     pieces = lax.all_to_all(pieces, every, split_axis=0, concat_axis=0, tiled=True)
     halos = exchange(faces)
     pieces, halos = lax.optimization_barrier((pieces, halos))
-    column = call(scale_kernel, struct(SZ, 2 * SZ), pieces)
+    column = call(scale_kernel, struct(SZ, 1, 2 * SZ), pieces)
     table = lax.all_to_all(column, every, split_axis=0, concat_axis=0, tiled=True)
     first, column = lax.optimization_barrier((first, column))
-    (new_velocity,) = section(gy, first, halos, weights, velocity)
+    (new_velocity,) = section(gy, first, halos, net, velocity)
     table, new_velocity = lax.optimization_barrier((table, new_velocity))
-    grad_mid, grad_in, rest = call(
-        final_kernel, [struct(SZ, SZ), struct(SZ, FEAT), struct(8, SZ)], table
-    )
-    return (new_velocity, grad_in, rest[1], grad_mid, rest[0], rest[2])
+    grad_mid, grad_in, grad_b_in, grad_b_mid, grad_out = call(
+        final_kernel,
+        [struct(HID, HID), struct(FEAT, HID), struct(1, HID), struct(1, HID), struct(1, HID)],
+        table.reshape(SZ, 2 * SZ),
+    )
+    return (
+        new_velocity, grad_in.T, grad_b_in.reshape(HID), grad_mid, grad_b_mid.reshape(HID),
+        grad_out.reshape(HID),
+    )
 
 
 def solution(mesh):

time: 148 us -> 126 us (0.85)
  Pallas kernels: 78.9 us -> 69.2 us
  local copies, waits for them, and re-layouts: 11.3 us -> 4.08 us
  starting transfers between devices: 49.8 us -> 46.7 us
  other arithmetic: 2.32 us -> 0 us
    pallas_call x2, Pallas kernels: 40.4 us -> 29.7 us  [section(): pl.pallas_call(lambda *refs: section_kernel(second, *refs), out_shape=out...]
    unnamed x58 -> x46, local copies, waits for them, and re-layouts: 6.34 us -> 3.41 us
    all_to_all x1, starting transfers between devices: 10.4 us -> 7.93 us  [on_device(): lax.all_to_all(pieces, every, split_axis=0, concat_axis=0, tiled=True)]
    pallas_call x3 -> x4, Pallas kernels: 5.08 us -> 6.94 us  [call(): pl.pallas_call(kernel, out_shape=outs, in_specs=whole(len(args)), out_spe...]
    all_to_all x1 -> x0, local copies, waits for them, and re-layouts: 1.71 us -> none  [on_device(): lax.all_to_all(column, every, split_axis=0, concat_axis=0, tiled=True)]
    concatenate x4 -> x0, other arithmetic: 1.55 us -> none  [the longest x1 0.79 us: prepare(): first_w = jnp.concatenate([first_w, pick], 1)]
  transfers between devices with their start and end apart: 15 -> 15, of which waited for: 2 -> 2; matrix products, arithmetic and copies ran while one was open for 3% -> 1% of each run, Pallas kernels for 27% -> 25%
where the time goes in v2:
time: 126 us; the launch traced here: 125 us
  Pallas kernels  69.2 us (55%)
  starting transfers between devices  46.7 us (37%)
  local copies, waits for them, and re-layouts  4.08 us (3%)
  waiting for transfers between devices  3.68 us (3%)
  between operations  1.58 us (1%)
    pallas_call x2, Pallas kernels, section(): pl.pallas_call(lambda *refs: section_kernel(second, *refs), out_shape=out...  29.7 us
    pallas_call x1, Pallas kernels, patch_grads(): pl.pallas_call(patch_kernel, out_shape=jax.ShapeDtypeStruct((4, TRAINERS,...  29.2 us
    ppermute x6, starting transfers between devices, shift(): lax.ppermute(high, axis, [(i, (i + 1) % count) for i in range(ends)])  15.4 us
    ppermute x6, starting transfers between devices, shift(): lax.ppermute(low, axis, [((i + 1) % count, i) for i in range(ends)])  9.2 us
    all_to_all x1, starting transfers between devices, on_device(): lax.all_to_all(pieces, every, split_axis=0, concat_axis=0, tiled=True)  7.93 us
    all_to_all x1, starting transfers between devices, on_device(): lax.all_to_all(column, every, split_axis=0, concat_axis=0, tiled=True)  7.38 us
    pallas_call x4, Pallas kernels, call(): pl.pallas_call(kernel, out_shape=outs, in_specs=whole(len(args)), out_spe...  6.94 us
    all_to_all x1, starting transfers between devices, on_device(): lax.all_to_all(grads.reshape(16, QROWS, SZ), ('gy', 'gz'), split_axis=0,...  6.77 us
  transfers between devices with their start and end apart: 15, of which 2 were waited for; matrix products, arithmetic and copies ran while one was open for 1% of the time, Pallas kernels for 25%

profile of v2, /device:TPU:1, one launch (start us, length us, event | category | flops | bytes accessed | tf_op | source)
XLA Modules:
  0.0 125.2 jit_solution(2180766734670018393)
XLA Ops:
  0.6 3.4 %faces.1 = (f32[3,32,128]{2,1,0:T(8,128)}, f32[3,32,128]{2,1,0:T(8,128)}, f32[3,16,128]{2,1,0:T(8,128)}, f32[3,16,128]{2,1,0:T(8,128)}, f32[32,128]{1,0:T(8,128)}, /*index=5*/f32[32,128]{1,0:T(8,128)}) custom-call(f32[3,16,32,128]{3,2,1,0:T(8,128)} %refs_8_.1), custom_call_target="tpu_custom_call" | custom-call | tf_op jit(solution)/shard_map/faces/pallas_call | solution.py:104
  4.0 3.6 %collective-permute-start = (f32[3,32,128]{2,1,0:T(8,128)}, f32[3,32,128]{2,1,0:T(8,128)S(1)}, u32[]{:S(2)}, u32[]{:S(2)}) collective-permute-start(f32[3,32,128]{2,1,0:T(8,128)} %get-tuple-element.42), channel_id=1, source_target_pairs={{0,16},{16,32},{32,48},{48,64},{64,80},{80,96},{96,112},{112,0},{1... | collective-permute-start | bytes 147464 | tf_op jit(solution)/shard_map/ppermute | solution.py:115
  7.5 3.5 %collective-permute-start.1 = (f32[3,32,128]{2,1,0:T(8,128)}, f32[3,32,128]{2,1,0:T(8,128)S(1)}, u32[]{:S(2)}, u32[]{:S(2)}) collective-permute-start(f32[3,32,128]{2,1,0:T(8,128)} %get-tuple-element.43), channel_id=1, source_target_pairs={{16,0},{32,16},{48,32},{64,48},{80,64},{96,80},{112,96},{0,112},{1... | collective-permute-start | bytes 147464 | tf_op jit(solution)/shard_map/ppermute | solution.py:116
  11.0 1.2 collective-permute-start.4
  12.2 3.2 %collective-permute-start.2 = (f32[3,16,128]{2,1,0:T(8,128)}, f32[3,16,128]{2,1,0:T(8,128)S(1)}, u32[]{:S(2)}, u32[]{:S(2)}) collective-permute-start(f32[3,16,128]{2,1,0:T(8,128)} %get-tuple-element.44), channel_id=1, source_target_pairs={{0,4},{4,8},{8,12},{1,5},{5,9},{9,13},{2,6},{6,10},{10,14},{3,7},{... | collective-permute-start | bytes 73736 | tf_op jit(solution)/shard_map/ppermute | solution.py:115
  15.4 1.3 %collective-permute-start.3 = (f32[3,16,128]{2,1,0:T(8,128)}, f32[3,16,128]{2,1,0:T(8,128)S(1)}, u32[]{:S(2)}, u32[]{:S(2)}) collective-permute-start(f32[3,16,128]{2,1,0:T(8,128)} %get-tuple-element.45), channel_id=1, source_target_pairs={{4,0},{8,4},{12,8},{5,1},{9,5},{13,9},{6,2},{10,6},{14,10},{7,3},{... | collective-permute-start | bytes 73736 | tf_op jit(solution)/shard_map/ppermute | solution.py:116
  16.7 0.0 collective-permute-done.4.hz0.refs_6_
  16.7 0.0 copy-start.6
  16.7 0.1 collective-permute-start.5
  17.6 0.0 copy-done.15
  17.6 0.7 copy.22
  18.2 0.0 copy-done.14
  18.2 0.7 copy.19.w_in
  19.0 0.0 copy-done.6
  19.0 1.9 %prepare_kernel.1 = (bf16[8,144,96]{2,1,0:T(8,128)(2,1)}, bf16[128,144]{1,0:T(8,128)(2,1)}, bf16[128,128]{1,0:T(8,128)(2,1)}, bf16[8,16,128]{2,1,0:T(8,128)(2,1)}, f32[128,128]{1,0:T(8,128)}) custom-call(bf16[128,10]{1,0:T(8,128)(2,1)} %copy.19.w_in, f32[1,128]{1,0:T(1,128)} %bitcast.25, bf16[128,128]{1,0:T(8,128)(2,1)} %w_mid.1, f32[1,128]{1,0:T(1,128)} %bitcast.26, ...), custom_call_target="tpu_custom_call" | custom-call | tf_op jit(solution)/shard_map/prepare_kernel/pallas_call | solution.py:504
  20.9 0.0 collective-permute-done.5.hz1.refs_7_
  20.9 0.0 collective-permute-done.2.hy0.refs_4_
  20.9 0.0 copy-start.4
  20.9 0.0 collective-permute-done.3.hy1.refs_5_
  20.9 0.0 copy-start.5
  20.9 0.0 collective-permute-done.hx0.refs_2_
  20.9 0.0 copy-start.2
  20.9 0.0 collective-permute-done.1.hx1.refs_3_
  20.9 0.0 copy-start.3
  20.9 0.5 copy-done.7
  21.5 0.0 copy-done.4
  21.5 0.0 copy-done.5
  21.5 0.0 copy-done.2
  21.5 0.0 copy-done.3
  21.6 29.2 %patch_grads.1 = f32[4,4,40,128]{3,2,1,0:T(8,128)} custom-call(s32[1]{0:T(128)} %bitcast.gy.refs_0_, s32[1]{0:T(128)} %bitcast.19.count, s32[8,3]{1,0:T(8,128)} %bitcast.24, s32[8]{0:T(128)} %bitcast.28, f32[3,16,32,128]{3,2,1,0:T(8,128)} %refs_8_.1, f32[3,32,128]{2,1,0:T(8,128)} %copy-done.2, f32[3,32,128]{2,1,0:T(8,128)} %copy-done.3, ...), custom_call_target="tpu_custom_call" | custom-call | tf_op jit(solution)/shard_map/patch_grads/pallas_call | solution.py:429
  50.7 6.8 %all-to-all-start = ((f32[16,40,128]{2,1,0:T(8,128)}), f32[16,40,128]{2,1,0:T(8,128)S(1)}, u32[]{:S(2)}, u32[]{:S(2)}) async-start(f32[16,40,128]{2,1,0:T(8,128)} %bitcast.20), calls=%async_computation | async-start | bytes 655360 | tf_op jit(solution)/shard_map/all_to_all | solution.py:577
  57.5 14.9 %section_one.1 = (f32[3,16,32,128]{3,2,1,0:T(8,128)}, f32[3,32,128]{2,1,0:T(8,128)}, f32[3,32,128]{2,1,0:T(8,128)}, f32[3,16,128]{2,1,0:T(8,128)}, f32[3,16,128]...) custom-call(s32[1]{0:T(128)} %bitcast.gy.refs_0_, f32[3,16,32,128]{3,2,1,0:T(8,128)} %refs_8_.1, ...), custom_call_target="tpu_custom_call" | custom-call | tf_op jit(solution)/shard_map/section_one/pallas_call | solution.py:251
  72.4 0.0 all-to-all-done.parts
  72.4 0.7 copy-done
  73.1 1.8 %gather_kernel.1 = f32[128,128]{1,0:T(8,128)} custom-call(f32[16,40,128]{2,1,0:T(8,128)} %copy-done), custom_call_target="tpu_custom_call" | custom-call | tf_op jit(solution)/shard_map/gather_kernel/pallas_call | solution.py:504
  74.9 7.9 %all-to-all-start.1 = ((f32[128,1,128]{2,1,0:T(1,128)}), f32[128,1,128]{2,1,0:T(1,128)S(1)}, u32[]{:S(2)}, u32[]{:S(2)}) async-start(f32[128,1,128]{2,1,0:T(1,128)} %bitcast.23), calls=%async_computation.1 | async-start | bytes 131072 | tf_op jit(solution)/shard_map/all_to_all | solution.py:584
  82.8 0.0 copy-done.17
  82.8 2.9 %collective-permute-start.6 = (f32[3,32,128]{2,1,0:T(8,128)S(1)}, f32[3,32,128]{2,1,0:T(8,128)S(1)}, u32[]{:S(2)}, u32[]{:S(2)}) collective-permute-start(f32[3,32,128]{2,1,0:T(8,128)S(1)} %copy-done.17), channel_id=1, source_target_pairs={{0,16},{16,32},{32,48},{48,64},{64,80},{80,96},{96,112},{112,0},{1... | collective-permute-start | bytes 147464 | tf_op jit(solution)/shard_map/ppermute | solution.py:115
  85.8 0.0 copy-done.16
  85.8 2.9 %collective-permute-start.7 = (f32[3,32,128]{2,1,0:T(8,128)S(1)}, f32[3,32,128]{2,1,0:T(8,128)S(1)}, u32[]{:S(2)}, u32[]{:S(2)}) collective-permute-start(f32[3,32,128]{2,1,0:T(8,128)S(1)} %copy-done.16), channel_id=1, source_target_pairs={{16,0},{32,16},{48,32},{64,48},{80,64},{96,80},{112,96},{0,112},{1... | collective-permute-start | bytes 147464 | tf_op jit(solution)/shard_map/ppermute | solution.py:116
  88.7 1.5 %collective-permute-start.10 = (f32[32,128]{1,0:T(8,128)S(1)}, f32[32,128]{1,0:T(8,128)S(1)}, u32[]{:S(2)}, u32[]{:S(2)}) collective-permute-start(f32[32,128]{1,0:T(8,128)S(1)} %copy-done.21), channel_id=1, source_target_pairs={{0,1},{1,2},{2,3},{3,0},{4,5},{5,6},{6,7},{7,4},{8,9},{9,10},{10,1... | collective-permute-start | bytes 49160 | tf_op jit(solution)/shard_map/ppermute | solution.py:115
  90.2 3.1 %collective-permute-start.8 = (f32[3,16,128]{2,1,0:T(8,128)S(1)}, f32[3,16,128]{2,1,0:T(8,128)S(1)}, u32[]{:S(2)}, u32[]{:S(2)}) collective-permute-start(f32[3,16,128]{2,1,0:T(8,128)S(1)} %copy-done.19), channel_id=1, source_target_pairs={{0,4},{4,8},{8,12},{1,5},{5,9},{9,13},{2,6},{6,10},{10,14},{3,7},{... | collective-permute-start | bytes 73736 | tf_op jit(solution)/shard_map/ppermute | solution.py:115
  93.3 0.0 copy-done.18
  93.3 1.3 %collective-permute-start.9 = (f32[3,16,128]{2,1,0:T(8,128)S(1)}, f32[3,16,128]{2,1,0:T(8,128)S(1)}, u32[]{:S(2)}, u32[]{:S(2)}) collective-permute-start(f32[3,16,128]{2,1,0:T(8,128)S(1)} %copy-done.18), channel_id=1, source_target_pairs={{4,0},{8,4},{12,8},{5,1},{9,5},{13,9},{6,2},{10,6},{14,10},{7,3},{... | collective-permute-start | bytes 73736 | tf_op jit(solution)/shard_map/ppermute | solution.py:116
  94.6 0.0 collective-permute-done.10.refs_6_
  94.6 0.1 collective-permute-start.11
  94.7 3.4 %collective-permute-done.11.refs_7_ = f32[32,128]{1,0:T(8,128)S(1)} collective-permute-done((f32[32,128]{1,0:T(8,128)S(1)}, f32[32,128]{1,0:T(8,128)S(1)}, u32[]{:S(2)}, u32[]{:S(2)}) %collective-permute-start.11) | collective-permute-done | bytes 16416 | tf_op jit(solution)/shard_map/ppermute | solution.py:116
  98.1 0.0 collective-permute-done.8.refs_4_
  98.1 0.2 collective-permute-done.9.refs_5_
  98.3 0.0 collective-permute-done.6.refs_2_
  98.4 0.0 collective-permute-done.7.refs_3_
  98.4 0.0 all-to-all-done.1
  98.4 0.0 copy-start.1
  98.4 0.6 copy-done.1
  99.0 1.7 %scale_kernel.1 = f32[128,1,256]{2,1,0:T(1,128)} custom-call(f32[128,128]{1,0:T(8,128)} %bitcast.22), custom_call_target="tpu_custom_call" | custom-call | tf_op jit(solution)/shard_map/scale_kernel/pallas_call | solution.py:504
  100.7 0.0 copy-done.10
  100.7 0.0 copy-done.11
  100.7 0.0 copy-done.8
  100.7 0.0 copy-done.9
  100.8 7.4 %all-to-all-start.2 = ((f32[128,1,256]{2,1,0:T(1,128)}), f32[128,1,256]{2,1,0:T(1,128)S(1)}, u32[]{:S(2)}, u32[]{:S(2)}) async-start(f32[128,1,256]{2,1,0:T(1,128)} %scale_kernel.1), calls=%async_computation.2 | async-start | bytes 262144 | tf_op jit(solution)/shard_map/all_to_all | solution.py:588
  108.1 14.8 %section_two.1 = f32[3,16,32,128]{3,2,1,0:T(8,128)} custom-call(s32[1]{0:T(128)} %bitcast.gy.refs_0_, f32[3,16,32,128]{3,2,1,0:T(8,128)} %get-tuple-element.64.refs_1_, f32[3,32,128]{2,1,0:T(8,128)} %copy-done.8, f32[3,32,128]{2,1,0:T(8,128)} %copy-done.9, f32[3,16,128]{2,1,0:T(8,128)} %copy-done.10, f32[3,16,128]{2,1,0:T(8,128)} %copy-done.11, ...), custom_call_target="tpu_custom_call" | custom-call | tf_op jit(solution)/shard_map/section_two/pallas_call | solution.py:251
  123.0 0.0 all-to-all-done.2
  123.0 0.7 copy.25
  123.6 1.6 %final_kernel.1 = (f32[128,128]{1,0:T(8,128)}, f32[10,128]{1,0:T(8,128)}, f32[1,128]{1,0:T(1,128)}, f32[1,128]{1,0:T(1,128)}, f32[1,128]{1,0:T(1,128)}) custom-call(f32[128,256]{1,0:T(8,128)} %bitcast.21), custom_call_target="tpu_custom_call" | custom-call | tf_op jit(solution)/shard_map/final_kernel/pallas_call | solution.py:504
  (21 shorter events, 0.0 us)
Async XLA Ops:
  4.0 16.9 %collective-permute-start = (f32[3,32,128]{2,1,0:T(8,128)}, f32[3,32,128]{2,1,0:T(8,128)S(1)}, u32[]{:S(2)}, u32[]{:S(2)}) collective-permute-start(f32[3,32,128]{2,1,0:T(8,128)} %get-tuple-element.42), channel_id=1, source_target_pairs={{0,16},{16,32},{32,48},{48,64},{64,80},{80,96},{96,112},{112,0},{1... | collective-permute-start | bytes 147464 | tf_op jit(solution)/shard_map/ppermute | solution.py:115
  7.5 13.4 %collective-permute-start.1 = (f32[3,32,128]{2,1,0:T(8,128)}, f32[3,32,128]{2,1,0:T(8,128)S(1)}, u32[]{:S(2)}, u32[]{:S(2)}) collective-permute-start(f32[3,32,128]{2,1,0:T(8,128)} %get-tuple-element.43), channel_id=1, source_target_pairs={{16,0},{32,16},{48,32},{64,48},{80,64},{96,80},{112,96},{0,112},{1... | collective-permute-start | bytes 147464 | tf_op jit(solution)/shard_map/ppermute | solution.py:116
  11.0 5.7 %collective-permute-start.4 = (f32[32,128]{1,0:T(8,128)}, f32[32,128]{1,0:T(8,128)S(1)}, u32[]{:S(2)}, u32[]{:S(2)}) collective-permute-start(f32[32,128]{1,0:T(8,128)} %get-tuple-element.46), channel_id=1, source_target_pairs={{0,1},{1,2},{2,3},{3,0},{4,5},{5,6},{6,7},{7,4},{8,9},{9,10},{10,1... | collective-permute-start | bytes 49160 | tf_op jit(solution)/shard_map/ppermute | solution.py:115
  12.2 8.7 %collective-permute-start.2 = (f32[3,16,128]{2,1,0:T(8,128)}, f32[3,16,128]{2,1,0:T(8,128)S(1)}, u32[]{:S(2)}, u32[]{:S(2)}) collective-permute-start(f32[3,16,128]{2,1,0:T(8,128)} %get-tuple-element.44), channel_id=1, source_target_pairs={{0,4},{4,8},{8,12},{1,5},{5,9},{9,13},{2,6},{6,10},{10,14},{3,7},{... | collective-permute-start | bytes 73736 | tf_op jit(solution)/shard_map/ppermute | solution.py:115
  15.4 5.5 %collective-permute-start.3 = (f32[3,16,128]{2,1,0:T(8,128)}, f32[3,16,128]{2,1,0:T(8,128)S(1)}, u32[]{:S(2)}, u32[]{:S(2)}) collective-permute-start(f32[3,16,128]{2,1,0:T(8,128)} %get-tuple-element.45), channel_id=1, source_target_pairs={{4,0},{8,4},{12,8},{5,1},{9,5},{13,9},{6,2},{10,6},{14,10},{7,3},{... | collective-permute-start | bytes 73736 | tf_op jit(solution)/shard_map/ppermute | solution.py:116
  16.7 2.3 %copy-start.6 = (f32[32,128]{1,0:T(8,128)}, f32[32,128]{1,0:T(8,128)S(1)}, u32[]{:S(2)}) copy-start(f32[32,128]{1,0:T(8,128)S(1)} %collective-permute-done.4.hz0.refs_6_) | copy-start | bytes 49156
  16.7 4.1 %collective-permute-start.5 = (f32[32,128]{1,0:T(8,128)}, f32[32,128]{1,0:T(8,128)S(1)}, u32[]{:S(2)}, u32[]{:S(2)}) collective-permute-start(f32[32,128]{1,0:T(8,128)} %get-tuple-element.47), channel_id=1, source_target_pairs={{1,0},{2,1},{3,2},{0,3},{5,4},{6,5},{7,6},{4,7},{9,8},{10,9},{11,1... | collective-permute-start | bytes 49160 | tf_op jit(solution)/shard_map/ppermute | solution.py:116
  16.9 0.7 copy-start.15
  16.9 1.4 %copy-start.14 = (bf16[128,10]{0,1:T(8,128)(2,1)S(1)}, bf16[128,10]{0,1:T(8,128)(2,1)}, u32[]{:S(2)}) copy-start(bf16[128,10]{0,1:T(8,128)(2,1)} %param.12) | copy-start | bytes 7684
  20.9 0.6 copy-start.7
  20.9 0.6 copy-start.4
  20.9 0.6 copy-start.5
  20.9 0.6 copy-start.2
  20.9 0.6 copy-start.3
  50.7 21.6 %all-to-all-start = ((f32[16,40,128]{2,1,0:T(8,128)}), f32[16,40,128]{2,1,0:T(8,128)S(1)}, u32[]{:S(2)}, u32[]{:S(2)}) async-start(f32[16,40,128]{2,1,0:T(8,128)} %bitcast.20), calls=%async_computation | async-start | bytes 655360 | tf_op jit(solution)/shard_map/all_to_all | solution.py:577
  72.4 0.7 copy-start
  73.1 15.6 %copy-start.21 = (f32[32,128]{1,0:T(8,128)S(1)}, f32[32,128]{1,0:T(8,128)}, u32[]{:S(2)}) copy-start(f32[32,128]{1,0:T(8,128)} %get-tuple-element.60) | copy-start | bytes 49156
  73.1 17.1 %copy-start.19 = (f32[3,16,128]{2,1,0:T(8,128)S(1)}, f32[3,16,128]{2,1,0:T(8,128)}, u32[]{:S(2)}) copy-start(f32[3,16,128]{2,1,0:T(8,128)} %get-tuple-element.58) | copy-start | bytes 73732
  74.9 8.0 %copy-start.17 = (f32[3,32,128]{2,1,0:T(8,128)S(1)}, f32[3,32,128]{2,1,0:T(8,128)}, u32[]{:S(2)}) copy-start(f32[3,32,128]{2,1,0:T(8,128)} %get-tuple-element.56) | copy-start | bytes 147460
  74.9 10.9 %copy-start.16 = (f32[3,32,128]{2,1,0:T(8,128)S(1)}, f32[3,32,128]{2,1,0:T(8,128)}, u32[]{:S(2)}) copy-start(f32[3,32,128]{2,1,0:T(8,128)} %get-tuple-element.57) | copy-start | bytes 147460
  74.9 18.4 %copy-start.18 = (f32[3,16,128]{2,1,0:T(8,128)S(1)}, f32[3,16,128]{2,1,0:T(8,128)}, u32[]{:S(2)}) copy-start(f32[3,16,128]{2,1,0:T(8,128)} %get-tuple-element.59) | copy-start | bytes 73732
  74.9 19.7 %copy-start.20 = (f32[32,128]{1,0:T(8,128)S(1)}, f32[32,128]{1,0:T(8,128)}, u32[]{:S(2)}) copy-start(f32[32,128]{1,0:T(8,128)} %get-tuple-element.61) | copy-start | bytes 49156
  74.9 23.5 %all-to-all-start.1 = ((f32[128,1,128]{2,1,0:T(1,128)}), f32[128,1,128]{2,1,0:T(1,128)S(1)}, u32[]{:S(2)}, u32[]{:S(2)}) async-start(f32[128,1,128]{2,1,0:T(1,128)} %bitcast.23), calls=%async_computation.1 | async-start | bytes 131072 | tf_op jit(solution)/shard_map/all_to_all | solution.py:584
  82.8 15.5 %collective-permute-start.6 = (f32[3,32,128]{2,1,0:T(8,128)S(1)}, f32[3,32,128]{2,1,0:T(8,128)S(1)}, u32[]{:S(2)}, u32[]{:S(2)}) collective-permute-start(f32[3,32,128]{2,1,0:T(8,128)S(1)} %copy-done.17), channel_id=1, source_target_pairs={{0,16},{16,32},{32,48},{48,64},{64,80},{80,96},{96,112},{112,0},{1... | collective-permute-start | bytes 147464 | tf_op jit(solution)/shard_map/ppermute | solution.py:115
  85.8 12.6 %collective-permute-start.7 = (f32[3,32,128]{2,1,0:T(8,128)S(1)}, f32[3,32,128]{2,1,0:T(8,128)S(1)}, u32[]{:S(2)}, u32[]{:S(2)}) collective-permute-start(f32[3,32,128]{2,1,0:T(8,128)S(1)} %copy-done.16), channel_id=1, source_target_pairs={{16,0},{32,16},{48,32},{64,48},{80,64},{96,80},{112,96},{0,112},{1... | collective-permute-start | bytes 147464 | tf_op jit(solution)/shard_map/ppermute | solution.py:116
  88.7 5.9 %collective-permute-start.10 = (f32[32,128]{1,0:T(8,128)S(1)}, f32[32,128]{1,0:T(8,128)S(1)}, u32[]{:S(2)}, u32[]{:S(2)}) collective-permute-start(f32[32,128]{1,0:T(8,128)S(1)} %copy-done.21), channel_id=1, source_target_pairs={{0,1},{1,2},{2,3},{3,0},{4,5},{5,6},{6,7},{7,4},{8,9},{9,10},{10,1... | collective-permute-start | bytes 49160 | tf_op jit(solution)/shard_map/ppermute | solution.py:115
  90.2 8.0 %collective-permute-start.8 = (f32[3,16,128]{2,1,0:T(8,128)S(1)}, f32[3,16,128]{2,1,0:T(8,128)S(1)}, u32[]{:S(2)}, u32[]{:S(2)}) collective-permute-start(f32[3,16,128]{2,1,0:T(8,128)S(1)} %copy-done.19), channel_id=1, source_target_pairs={{0,4},{4,8},{8,12},{1,5},{5,9},{9,13},{2,6},{6,10},{10,14},{3,7},{... | collective-permute-start | bytes 73736 | tf_op jit(solution)/shard_map/ppermute | solution.py:115
  93.3 5.1 %collective-permute-start.9 = (f32[3,16,128]{2,1,0:T(8,128)S(1)}, f32[3,16,128]{2,1,0:T(8,128)S(1)}, u32[]{:S(2)}, u32[]{:S(2)}) collective-permute-start(f32[3,16,128]{2,1,0:T(8,128)S(1)} %copy-done.18), channel_id=1, source_target_pairs={{4,0},{8,4},{12,8},{5,1},{9,5},{13,9},{6,2},{10,6},{14,10},{7,3},{... | collective-permute-start | bytes 73736 | tf_op jit(solution)/shard_map/ppermute | solution.py:116
  94.6 6.1 %copy-start.12 = (f32[32,128]{1,0:T(8,128)}, f32[32,128]{1,0:T(8,128)S(1)}, u32[]{:S(2)}) copy-start(f32[32,128]{1,0:T(8,128)S(1)} %collective-permute-done.10.refs_6_) | copy-start | bytes 49156
  94.6 3.5 %collective-permute-start.11 = (f32[32,128]{1,0:T(8,128)S(1)}, f32[32,128]{1,0:T(8,128)S(1)}, u32[]{:S(2)}, u32[]{:S(2)}) collective-permute-start(f32[32,128]{1,0:T(8,128)S(1)} %copy-done.20), channel_id=1, source_target_pairs={{1,0},{2,1},{3,2},{0,3},{5,4},{6,5},{7,6},{4,7},{9,8},{10,9},{11,1... | collective-permute-start | bytes 49160 | tf_op jit(solution)/shard_map/ppermute | solution.py:116
  98.1 2.6 %copy-start.13 = (f32[32,128]{1,0:T(8,128)}, f32[32,128]{1,0:T(8,128)S(1)}, u32[]{:S(2)}) copy-start(f32[32,128]{1,0:T(8,128)S(1)} %collective-permute-done.11.refs_7_) | copy-start | bytes 49156
  98.1 2.6 %copy-start.10 = (f32[3,16,128]{2,1,0:T(8,128)}, f32[3,16,128]{2,1,0:T(8,128)S(1)}, u32[]{:S(2)}) copy-start(f32[3,16,128]{2,1,0:T(8,128)S(1)} %collective-permute-done.8.refs_4_) | copy-start | bytes 73732
  98.3 2.4 %copy-start.11 = (f32[3,16,128]{2,1,0:T(8,128)}, f32[3,16,128]{2,1,0:T(8,128)S(1)}, u32[]{:S(2)}) copy-start(f32[3,16,128]{2,1,0:T(8,128)S(1)} %collective-permute-done.9.refs_5_) | copy-start | bytes 73732
  98.3 2.4 %copy-start.8 = (f32[3,32,128]{2,1,0:T(8,128)}, f32[3,32,128]{2,1,0:T(8,128)S(1)}, u32[]{:S(2)}) copy-start(f32[3,32,128]{2,1,0:T(8,128)S(1)} %collective-permute-done.6.refs_2_) | copy-start | bytes 147460
  98.4 2.4 %copy-start.9 = (f32[3,32,128]{2,1,0:T(8,128)}, f32[3,32,128]{2,1,0:T(8,128)S(1)}, u32[]{:S(2)}) copy-start(f32[3,32,128]{2,1,0:T(8,128)S(1)} %collective-permute-done.7.refs_3_) | copy-start | bytes 147460
  98.4 0.6 copy-start.1
  100.8 22.2 %all-to-all-start.2 = ((f32[128,1,256]{2,1,0:T(1,128)}), f32[128,1,256]{2,1,0:T(1,128)S(1)}, u32[]{:S(2)}, u32[]{:S(2)}) async-start(f32[128,1,256]{2,1,0:T(1,128)} %scale_kernel.1), calls=%async_computation.2 | async-start | bytes 262144 | tf_op jit(solution)/shard_map/all_to_all | solution.py:588
